TPU v7x, 128 devices: a whole 4x4x4 slice. The times are simulated.
128 devices in a mesh: gx: 8 (over y, core), gy: 4 (over z), gz: 4 (over x).
Axes of the slice: x: 4, y: 4, z: 4, core: 2. Of those that a mesh axis runs over, the one named last changes fastest.
Arguments:
- source_field: bfloat16 [2, 2, 16, 512, 2048], P(None, None, 'gz', 'gy', 'gx'), may hold values from -6 to 6
- adjoint_source: bfloat16 [2, 2, 16, 512, 2048], P(None, None, 'gz', 'gy', 'gx'), may hold values from -6 to 6
- x_inverse: bfloat16 [8, 4, 2, 256, 256], P('gx', 'gy'), may hold values from -1 to 1.25
- y_inverse: bfloat16 [8, 4, 2, 128, 128], P('gx', 'gy'), may hold values from -1 to 1.25
Outputs:
- state_field: bfloat16 [2, 2, 16, 512, 2048], P(None, None, 'gz', 'gy', 'gx')
- adjoint_field: bfloat16 [2, 2, 16, 512, 2048], P(None, None, 'gz', 'gy', 'gx')
- gradient: float32 [16, 512, 2048], P('gz', 'gy', 'gx')
All inputs are finite; a program needn't handle non-finite values.
Results may differ from a plain program's by a relative error of at most 0.017.
Values may be sent and summed in bfloat16 or wider, within the bound.
A program may use at most 64 MiB of HBM per device.

v0:
```python
import jax
import jax.numpy as jnp
from jax import lax
from jax.sharding import PartitionSpec as P


def passed_along(value, axis, steps):
    count = lax.axis_size(axis)
    leading, last = (max(0, -steps), min(count, count - steps))
    return lax.ppermute(value, axis, [(source, source + steps) for source in range(leading, last)])


def extended(cells, sides, width):
    for axis, dim in sides:
        count = lax.axis_size(axis)
        ends = count - 1
        head = lax.slice_in_dim(cells, 0, width, axis=dim)
        tail = lax.slice_in_dim(cells, cells.shape[dim] - width, cells.shape[dim], axis=dim)
        cells = jnp.concatenate(
            [
                lax.ppermute(tail, axis, [(i, (i + 1) % count) for i in range(ends)]),
                cells,
                lax.ppermute(head, axis, [((i + 1) % count, i) for i in range(ends)]),
            ],
            axis=dim,
        )
    return cells


def combine_parts(real_term, imag_term):
    real_out = real_term[:, 0] - imag_term[:, 1]
    imag_out = imag_term[:, 0] + real_term[:, 1]
    return jnp.stack([real_out, imag_out], axis=1).astype(jnp.bfloat16)


def solve_along_x(field, real_matrix, imag_matrix, form):
    real_term = jnp.einsum(form, field, real_matrix, preferred_element_type=jnp.float32)
    imag_term = jnp.einsum(form, field, imag_matrix, preferred_element_type=jnp.float32)
    return combine_parts(real_term, imag_term)


def solve_along_y(field, real_matrix, imag_matrix, form):
    real_term = jnp.einsum(form, real_matrix, field, preferred_element_type=jnp.float32)
    imag_term = jnp.einsum(form, imag_matrix, field, preferred_element_type=jnp.float32)
    return combine_parts(real_term, imag_term)


def per_device(source_field, adjoint_source, x_inverse, y_inverse):
    shot_count = source_field.shape[0]
    depth_cells = source_field.shape[2]
    row_count = source_field.shape[3]
    line_cells = source_field.shape[4]
    lateral_row = lax.axis_index("gx")
    lateral_column = lax.axis_index("gy")
    rows_total = lax.axis_size("gx")
    columns_total = lax.axis_size("gy")
    fronts = rows_total + columns_total - 1
    x_real = x_inverse[0, 0, 0]
    x_imag = x_inverse[0, 0, 1]
    y_real = y_inverse[0, 0, 0]
    y_imag = y_inverse[0, 0, 1]
    state_front = lateral_row + lateral_column
    adjoint_front = rows_total - 1 - lateral_row + (columns_total - 1 - lateral_column)
    x_cells = lax.broadcasted_iota(jnp.int32, (1, 1, 1, 1, line_cells), 4)
    y_cells = lax.broadcasted_iota(jnp.int32, (1, 1, 1, row_count, 1), 3)
    first_column = (x_cells == 0).astype(jnp.float32)
    last_column = (x_cells == line_cells - 1).astype(jnp.float32)
    first_row = (y_cells == 0).astype(jnp.float32)
    last_row = (y_cells == row_count - 1).astype(jnp.float32)

    def state_solve(block, east_in, north_in):
        rhs_value = (
            block.astype(jnp.float32) + east_in.astype(jnp.float32)[..., None] * first_column
        )
        rhs_value = rhs_value + north_in.astype(jnp.float32)[:, :, :, None, :] * first_row
        half_value = solve_along_x(
            rhs_value.astype(jnp.bfloat16), x_real, x_imag, "bcdyx,wx->bcdyw"
        )
        return solve_along_y(half_value, y_real, y_imag, "py,bcdyx->bcdpx")

    def adjoint_solve(block, west_in, south_in):
        rhs_value = block.astype(jnp.float32) + west_in.astype(jnp.float32)[..., None] * last_column
        rhs_value = rhs_value + south_in.astype(jnp.float32)[:, :, :, None, :] * last_row
        half_value = solve_along_x(
            rhs_value.astype(jnp.bfloat16), x_real, x_imag, "bcdyx,xw->bcdyw"
        )
        return solve_along_y(half_value, y_real, y_imag, "yp,bcdyx->bcdpx")

    def hand_over(state_done, adjoint_done):
        east_in = passed_along(state_done[..., line_cells - 1], ("gx", "gy"), columns_total)
        north_in = passed_along(state_done[:, :, :, row_count - 1, :], "gy", 1)
        west_in = passed_along(adjoint_done[..., 0], ("gx", "gy"), -columns_total)
        south_in = passed_along(adjoint_done[:, :, :, 0, :], "gy", -1)
        return (east_in, north_in, west_in, south_in)

    def advance(section_index, loop_state):
        state_field, adjoint_field, east_in, north_in, west_in, south_in = loop_state
        state_active = state_front == section_index
        adjoint_active = adjoint_front == section_index
        state_new = state_solve(source_field, east_in, north_in)
        adjoint_new = adjoint_solve(adjoint_source, west_in, south_in)
        state_field = jnp.where(state_active, state_new, state_field)
        adjoint_field = jnp.where(adjoint_active, adjoint_new, adjoint_field)
        return (state_field, adjoint_field) + hand_over(state_field, adjoint_field)

    column_zeros = jnp.zeros((shot_count, 2, depth_cells, row_count), jnp.bfloat16)
    row_zeros = jnp.zeros((shot_count, 2, depth_cells, line_cells), jnp.bfloat16)
    initial = (
        jnp.zeros_like(source_field),
        jnp.zeros_like(adjoint_source),
        column_zeros,
        row_zeros,
        column_zeros,
        row_zeros,
    )
    finished = lax.fori_loop(0, fronts, advance, initial)
    stacked = jnp.stack([finished[0], finished[1]])
    padded = extended(stacked, (("gz", 3),), 1)
    centre = padded[:, :, :, 1:-1].astype(jnp.float32)
    above = padded[:, :, :, :-2].astype(jnp.float32)
    below = padded[:, :, :, 2:].astype(jnp.float32)
    blended = (0.5 * centre + 0.25 * (above + below)).astype(jnp.bfloat16)
    state_out = blended[0]
    adjoint_out = blended[1]
    state_wide = state_out.astype(jnp.float32)
    adjoint_wide = adjoint_out.astype(jnp.float32)
    product = state_wide[:, 0] * adjoint_wide[:, 0] - state_wide[:, 1] * adjoint_wide[:, 1]
    gradient = jnp.sum(product, axis=0) / shot_count
    return (state_out, adjoint_out, gradient)


def solution(mesh):
    in_specs = (
        P(None, None, "gz", "gy", "gx"),
        P(None, None, "gz", "gy", "gx"),
        P("gx", "gy", None, None, None),
        P("gx", "gy", None, None, None),
    )
    out_specs = (
        P(None, None, "gz", "gy", "gx"),
        P(None, None, "gz", "gy", "gx"),
        P("gz", "gy", "gx"),
    )
    return jax.shard_map(
        per_device, mesh=mesh, in_specs=in_specs, out_specs=out_specs, check_vma=False
    )
```

profile of v0, /device:TPU:1, one launch (start us, length us, event | category | flops | bytes accessed | tf_op | source)
XLA Modules:
  0.0 295.5 jit_solution(12238937155177304483)
XLA Ops:
  2.5 269.9 %while.24 = (s32[]{:T(128)}, bf16[2,2,4,128,256]{3,4,2,1,0:T(8,128)(2,1)S(1)}, bf16[2,2,4,128,256]{3,4,2,1,0:T(8,128)(2,1)S(1)}, bf16[2,2,4,128]{3,2,1,0:T(4,128...) while((s32[]{:T(128)}, ...), condition=%wide.region_1.2_spmd.clone, body=%wide.region_0.1_spmd.clone.sunk | while | flops 1632646656 | bytes 70206920 | solution.py:116
  2.6 1.9 fusion.68
  7.7 4.4 %collective-permute-start.1 = (bf16[2,2,4,256]{3,2,1,0:T(4,128)(2,1)S(1)}, bf16[2,2,4,256]{3,2,1,0:T(4,128)(2,1)S(1)}, u32[]{:S(2)}, u32[]{:S(2)}) collective-permute-start(bf16[2,2,4,256]{3,2,1,0:T(4,128)(2,1)S(1)} %slice_reduce_fusion.4), channel_id=1, source_target_pairs={{0,4},{4,8},{8,12},{1,5},{5,9},{9,13},{2,6},{6,10},{10,14},{3,7},{... | collective-permute-start | bytes 24584 | tf_op jit(solution)/shard_map/while/body/eval_jaxpr/ppermute | solution.py:10
  14.3 1.8 convolution_bitcast_fusion.10
  19.8 4.0 %collective-permute-start = (bf16[2,2,4,128]{3,2,1,0:T(4,128)(2,1)S(1)}, bf16[2,2,4,128]{3,2,1,0:T(4,128)(2,1)S(1)}, u32[]{:S(2)}, u32[]{:S(2)}) collective-permute-start(bf16[2,2,4,128]{3,2,1,0:T(4,128)(2,1)S(1)} %bitcast.104), channel_id=1, source_target_pairs={{0,16},{4,20},{8,24},{12,28},{16,32},{20,36},{24,40},{28,44},{32,4... | collective-permute-start | bytes 12296 | tf_op jit(solution)/shard_map/while/body/eval_jaxpr/ppermute | solution.py:10
  23.9 1.9 collective-permute-start.2
  25.8 3.0 %collective-permute-done.2 = bf16[2,2,4,128]{3,2,1,0:T(4,128)(2,1)S(1)} collective-permute-done((bf16[2,2,4,128]{3,2,1,0:T(4,128)(2,1)S(1)}, bf16[2,2,4,128]{3,2,1,0:T(4,128)(2,1)S(1)}, u32[]{:S(2)}, u32[]{:S(2)}) %collective-permute-start.2) | collective-permute-done | bytes 4128 | tf_op jit(solution)/shard_map/while/body/eval_jaxpr/ppermute | solution.py:10
  28.9 1.9 fusion.68
  34.0 4.3 %collective-permute-start.1 = (bf16[2,2,4,256]{3,2,1,0:T(4,128)(2,1)S(1)}, bf16[2,2,4,256]{3,2,1,0:T(4,128)(2,1)S(1)}, u32[]{:S(2)}, u32[]{:S(2)}) collective-permute-start(bf16[2,2,4,256]{3,2,1,0:T(4,128)(2,1)S(1)} %slice_reduce_fusion.4), channel_id=1, source_target_pairs={{0,4},{4,8},{8,12},{1,5},{5,9},{9,13},{2,6},{6,10},{10,14},{3,7},{... | collective-permute-start | bytes 24584 | tf_op jit(solution)/shard_map/while/body/eval_jaxpr/ppermute | solution.py:10
  40.4 1.8 convolution_bitcast_fusion.10
  45.9 2.2 collective-permute-start
  48.2 2.1 collective-permute-start.2
  50.3 2.8 collective-permute-done.2
  53.2 1.9 fusion.68
  58.3 4.3 %collective-permute-start.1 = (bf16[2,2,4,256]{3,2,1,0:T(4,128)(2,1)S(1)}, bf16[2,2,4,256]{3,2,1,0:T(4,128)(2,1)S(1)}, u32[]{:S(2)}, u32[]{:S(2)}) collective-permute-start(bf16[2,2,4,256]{3,2,1,0:T(4,128)(2,1)S(1)} %slice_reduce_fusion.4), channel_id=1, source_target_pairs={{0,4},{4,8},{8,12},{1,5},{5,9},{9,13},{2,6},{6,10},{10,14},{3,7},{... | collective-permute-start | bytes 24584 | tf_op jit(solution)/shard_map/while/body/eval_jaxpr/ppermute | solution.py:10
  70.3 2.2 collective-permute-start
  72.6 2.1 collective-permute-start.2
  74.7 2.8 collective-permute-done.2
  77.6 1.9 fusion.68
  82.7 4.3 %collective-permute-start.1 = (bf16[2,2,4,256]{3,2,1,0:T(4,128)(2,1)S(1)}, bf16[2,2,4,256]{3,2,1,0:T(4,128)(2,1)S(1)}, u32[]{:S(2)}, u32[]{:S(2)}) collective-permute-start(bf16[2,2,4,256]{3,2,1,0:T(4,128)(2,1)S(1)} %slice_reduce_fusion.4), channel_id=1, source_target_pairs={{0,4},{4,8},{8,12},{1,5},{5,9},{9,13},{2,6},{6,10},{10,14},{3,7},{... | collective-permute-start | bytes 24584 | tf_op jit(solution)/shard_map/while/body/eval_jaxpr/ppermute | solution.py:10
  94.7 2.2 collective-permute-start
  96.9 2.1 collective-permute-start.2
  99.1 2.8 collective-permute-done.2
  101.9 1.9 fusion.68
  107.1 4.3 %collective-permute-start.1 = (bf16[2,2,4,256]{3,2,1,0:T(4,128)(2,1)S(1)}, bf16[2,2,4,256]{3,2,1,0:T(4,128)(2,1)S(1)}, u32[]{:S(2)}, u32[]{:S(2)}) collective-permute-start(bf16[2,2,4,256]{3,2,1,0:T(4,128)(2,1)S(1)} %slice_reduce_fusion.4), channel_id=1, source_target_pairs={{0,4},{4,8},{8,12},{1,5},{5,9},{9,13},{2,6},{6,10},{10,14},{3,7},{... | collective-permute-start | bytes 24584 | tf_op jit(solution)/shard_map/while/body/eval_jaxpr/ppermute | solution.py:10
  113.5 1.8 convolution_bitcast_fusion.10
  119.0 2.2 collective-permute-start
  121.3 2.1 collective-permute-start.2
  123.4 2.8 collective-permute-done.2
  126.3 1.9 fusion.68
  131.4 4.3 %collective-permute-start.1 = (bf16[2,2,4,256]{3,2,1,0:T(4,128)(2,1)S(1)}, bf16[2,2,4,256]{3,2,1,0:T(4,128)(2,1)S(1)}, u32[]{:S(2)}, u32[]{:S(2)}) collective-permute-start(bf16[2,2,4,256]{3,2,1,0:T(4,128)(2,1)S(1)} %slice_reduce_fusion.4), channel_id=1, source_target_pairs={{0,4},{4,8},{8,12},{1,5},{5,9},{9,13},{2,6},{6,10},{10,14},{3,7},{... | collective-permute-start | bytes 24584 | tf_op jit(solution)/shard_map/while/body/eval_jaxpr/ppermute | solution.py:10
  143.4 2.2 collective-permute-start
  145.7 2.1 collective-permute-start.2
  147.8 2.8 collective-permute-done.2
  150.7 1.9 fusion.68
  155.8 4.3 %collective-permute-start.1 = (bf16[2,2,4,256]{3,2,1,0:T(4,128)(2,1)S(1)}, bf16[2,2,4,256]{3,2,1,0:T(4,128)(2,1)S(1)}, u32[]{:S(2)}, u32[]{:S(2)}) collective-permute-start(bf16[2,2,4,256]{3,2,1,0:T(4,128)(2,1)S(1)} %slice_reduce_fusion.4), channel_id=1, source_target_pairs={{0,4},{4,8},{8,12},{1,5},{5,9},{9,13},{2,6},{6,10},{10,14},{3,7},{... | collective-permute-start | bytes 24584 | tf_op jit(solution)/shard_map/while/body/eval_jaxpr/ppermute | solution.py:10
  167.8 2.2 collective-permute-start
  170.0 2.1 collective-permute-start.2
  172.1 2.8 collective-permute-done.2
  175.0 1.9 fusion.68
  180.1 4.3 %collective-permute-start.1 = (bf16[2,2,4,256]{3,2,1,0:T(4,128)(2,1)S(1)}, bf16[2,2,4,256]{3,2,1,0:T(4,128)(2,1)S(1)}, u32[]{:S(2)}, u32[]{:S(2)}) collective-permute-start(bf16[2,2,4,256]{3,2,1,0:T(4,128)(2,1)S(1)} %slice_reduce_fusion.4), channel_id=1, source_target_pairs={{0,4},{4,8},{8,12},{1,5},{5,9},{9,13},{2,6},{6,10},{10,14},{3,7},{... | collective-permute-start | bytes 24584 | tf_op jit(solution)/shard_map/while/body/eval_jaxpr/ppermute | solution.py:10
  192.1 2.2 collective-permute-start
  194.4 2.1 collective-permute-start.2
  196.5 2.8 collective-permute-done.2
  199.4 1.9 fusion.68
  204.5 4.3 %collective-permute-start.1 = (bf16[2,2,4,256]{3,2,1,0:T(4,128)(2,1)S(1)}, bf16[2,2,4,256]{3,2,1,0:T(4,128)(2,1)S(1)}, u32[]{:S(2)}, u32[]{:S(2)}) collective-permute-start(bf16[2,2,4,256]{3,2,1,0:T(4,128)(2,1)S(1)} %slice_reduce_fusion.4), channel_id=1, source_target_pairs={{0,4},{4,8},{8,12},{1,5},{5,9},{9,13},{2,6},{6,10},{10,14},{3,7},{... | collective-permute-start | bytes 24584 | tf_op jit(solution)/shard_map/while/body/eval_jaxpr/ppermute | solution.py:10
  211.0 1.8 convolution_bitcast_fusion.10
  216.5 2.2 collective-permute-start
  218.8 2.1 collective-permute-start.2
  220.9 2.8 collective-permute-done.2
  223.7 1.9 fusion.68
  228.9 4.3 %collective-permute-start.1 = (bf16[2,2,4,256]{3,2,1,0:T(4,128)(2,1)S(1)}, bf16[2,2,4,256]{3,2,1,0:T(4,128)(2,1)S(1)}, u32[]{:S(2)}, u32[]{:S(2)}) collective-permute-start(bf16[2,2,4,256]{3,2,1,0:T(4,128)(2,1)S(1)} %slice_reduce_fusion.4), channel_id=1, source_target_pairs={{0,4},{4,8},{8,12},{1,5},{5,9},{9,13},{2,6},{6,10},{10,14},{3,7},{... | collective-permute-start | bytes 24584 | tf_op jit(solution)/shard_map/while/body/eval_jaxpr/ppermute | solution.py:10
  240.8 2.2 collective-permute-start
  243.1 2.1 collective-permute-start.2
  245.2 2.8 collective-permute-done.2
  248.1 1.9 fusion.68
  253.2 4.3 %collective-permute-start.1 = (bf16[2,2,4,256]{3,2,1,0:T(4,128)(2,1)S(1)}, bf16[2,2,4,256]{3,2,1,0:T(4,128)(2,1)S(1)}, u32[]{:S(2)}, u32[]{:S(2)}) collective-permute-start(bf16[2,2,4,256]{3,2,1,0:T(4,128)(2,1)S(1)} %slice_reduce_fusion.4), channel_id=1, source_target_pairs={{0,4},{4,8},{8,12},{1,5},{5,9},{9,13},{2,6},{6,10},{10,14},{3,7},{... | collective-permute-start | bytes 24584 | tf_op jit(solution)/shard_map/while/body/eval_jaxpr/ppermute | solution.py:10
  265.2 2.2 collective-permute-start
  267.5 2.1 collective-permute-start.2
  269.6 2.8 collective-permute-done.2
  273.6 3.1 %collective-permute-start.4 = (bf16[2,2,2,1,128,256]{5,4,3,2,1,0:T(8,128)(2,1)S(1)}, bf16[2,2,2,1,128,256]{5,4,3,2,1,0:T(8,128)(2,1)S(1)}, u32[]{:S(2)}, u32[]{:S(2)}) collective-permute-start(bf16[2,2,2,1,128,256]{5,4,3,2,1,0:T(8,128)(2,1)S(1)} %get-tuple-element.410), channel_id=1, source_target_pairs={{0,1},{1,2},{2,3},{4,5},{5,6},{6,7},{8,9},{9,10},{10,11},{12,13},{... | collective-permute-start | bytes 1572872 | tf_op jit(solution)/shard_map/ppermute | solution.py:21
  278.0 9.2 %collective-permute-done.4 = bf16[2,2,2,1,128,256]{5,4,3,2,1,0:T(8,128)(2,1)S(1)} collective-permute-done((bf16[2,2,2,1,128,256]{5,4,3,2,1,0:T(8,128)(2,1)S(1)}, bf16[2,2,2,1,128,256]{5,4,3,2,1,0:T(8,128)(2,1)S(1)}, u32[]{:S(2)}, u32[]{:S(2)}) %collective-permute-start.4) | collective-permute-done | bytes 524320 | tf_op jit(solution)/shard_map/ppermute | solution.py:21
  287.2 4.1 %collective-permute-done.5 = bf16[2,2,2,1,128,256]{5,4,3,2,1,0:T(8,128)(2,1)S(1)} collective-permute-done((bf16[2,2,2,1,128,256]{5,4,3,2,1,0:T(8,128)(2,1)S(1)}, bf16[2,2,2,1,128,256]{5,4,3,2,1,0:T(8,128)(2,1)S(1)}, u32[]{:S(2)}, u32[]{:S(2)}) %collective-permute-start.5) | collective-permute-done | bytes 524320 | tf_op jit(solution)/shard_map/ppermute | solution.py:23
  292.5 1.9 fusion.39
  (440 shorter events, 118.2 us)
Async XLA Ops:
  6.7 5.4 %copy-start.3 = (bf16[2,2,4,128,256]{4,3,2,1,0:T(8,128)(2,1)S(1)}, bf16[2,2,4,128,256]{4,3,2,1,0:T(8,128)(2,1)}, u32[]{:S(2)}) copy-start(bf16[2,2,4,128,256]{4,3,2,1,0:T(8,128)(2,1)} %get-tuple-element.571) | copy-start | bytes 3145732 | tf_op jit(solution)/shard_map/while
  7.0 5.7 %copy-start = (bf16[2,2,4,128,256]{3,4,2,1,0:T(8,128)(2,1)}, bf16[2,2,4,128,256]{3,4,2,1,0:T(8,128)(2,1)S(1)}, u32[]{:S(2)}) copy-start(bf16[2,2,4,128,256]{3,4,2,1,0:T(8,128)(2,1)S(1)} %maximum_select_fusion.4) | copy-start | bytes 3145732 | tf_op jit(solution)/shard_map/while
  7.7 21.1 %collective-permute-start.1 = (bf16[2,2,4,256]{3,2,1,0:T(4,128)(2,1)S(1)}, bf16[2,2,4,256]{3,2,1,0:T(4,128)(2,1)S(1)}, u32[]{:S(2)}, u32[]{:S(2)}) collective-permute-start(bf16[2,2,4,256]{3,2,1,0:T(4,128)(2,1)S(1)} %slice_reduce_fusion.4), channel_id=1, source_target_pairs={{0,4},{4,8},{8,12},{1,5},{5,9},{9,13},{2,6},{6,10},{10,14},{3,7},{... | collective-permute-start | bytes 24584 | tf_op jit(solution)/shard_map/while/body/eval_jaxpr/ppermute | solution.py:10
  18.4 10.4 %collective-permute-start.3 = (bf16[2,2,4,256]{3,2,1,0:T(4,128)(2,1)S(1)}, bf16[2,2,4,256]{3,2,1,0:T(4,128)(2,1)S(1)}, u32[]{:S(2)}, u32[]{:S(2)}) collective-permute-start(bf16[2,2,4,256]{3,2,1,0:T(4,128)(2,1)S(1)} %slice_reduce_fusion.5), channel_id=1, source_target_pairs={{4,0},{8,4},{12,8},{5,1},{9,5},{13,9},{6,2},{10,6},{14,10},{7,3},{... | collective-permute-start | bytes 24584 | tf_op jit(solution)/shard_map/while/body/eval_jaxpr/ppermute | solution.py:10
  19.8 6.0 %collective-permute-start = (bf16[2,2,4,128]{3,2,1,0:T(4,128)(2,1)S(1)}, bf16[2,2,4,128]{3,2,1,0:T(4,128)(2,1)S(1)}, u32[]{:S(2)}, u32[]{:S(2)}) collective-permute-start(bf16[2,2,4,128]{3,2,1,0:T(4,128)(2,1)S(1)} %bitcast.104), channel_id=1, source_target_pairs={{0,16},{4,20},{8,24},{12,28},{16,32},{20,36},{24,40},{28,44},{32,4... | collective-permute-start | bytes 12296 | tf_op jit(solution)/shard_map/while/body/eval_jaxpr/ppermute | solution.py:10
  23.9 4.9 %collective-permute-start.2 = (bf16[2,2,4,128]{3,2,1,0:T(4,128)(2,1)S(1)}, bf16[2,2,4,128]{3,2,1,0:T(4,128)(2,1)S(1)}, u32[]{:S(2)}, u32[]{:S(2)}) collective-permute-start(bf16[2,2,4,128]{3,2,1,0:T(4,128)(2,1)S(1)} %bitcast.105), channel_id=1, source_target_pairs={{16,0},{20,4},{24,8},{28,12},{32,16},{36,20},{40,24},{44,28},{48,3... | collective-permute-start | bytes 12296 | tf_op jit(solution)/shard_map/while/body/eval_jaxpr/ppermute | solution.py:10
  33.0 5.3 %copy-start.3 = (bf16[2,2,4,128,256]{4,3,2,1,0:T(8,128)(2,1)S(1)}, bf16[2,2,4,128,256]{4,3,2,1,0:T(8,128)(2,1)}, u32[]{:S(2)}) copy-start(bf16[2,2,4,128,256]{4,3,2,1,0:T(8,128)(2,1)} %get-tuple-element.571) | copy-start | bytes 3145732 | tf_op jit(solution)/shard_map/while
  33.2 5.6 %copy-start = (bf16[2,2,4,128,256]{3,4,2,1,0:T(8,128)(2,1)}, bf16[2,2,4,128,256]{3,4,2,1,0:T(8,128)(2,1)S(1)}, u32[]{:S(2)}) copy-start(bf16[2,2,4,128,256]{3,4,2,1,0:T(8,128)(2,1)S(1)} %maximum_select_fusion.4) | copy-start | bytes 3145732 | tf_op jit(solution)/shard_map/while
  34.0 19.2 %collective-permute-start.1 = (bf16[2,2,4,256]{3,2,1,0:T(4,128)(2,1)S(1)}, bf16[2,2,4,256]{3,2,1,0:T(4,128)(2,1)S(1)}, u32[]{:S(2)}, u32[]{:S(2)}) collective-permute-start(bf16[2,2,4,256]{3,2,1,0:T(4,128)(2,1)S(1)} %slice_reduce_fusion.4), channel_id=1, source_target_pairs={{0,4},{4,8},{8,12},{1,5},{5,9},{9,13},{2,6},{6,10},{10,14},{3,7},{... | collective-permute-start | bytes 24584 | tf_op jit(solution)/shard_map/while/body/eval_jaxpr/ppermute | solution.py:10
  44.6 8.5 %collective-permute-start.3 = (bf16[2,2,4,256]{3,2,1,0:T(4,128)(2,1)S(1)}, bf16[2,2,4,256]{3,2,1,0:T(4,128)(2,1)S(1)}, u32[]{:S(2)}, u32[]{:S(2)}) collective-permute-start(bf16[2,2,4,256]{3,2,1,0:T(4,128)(2,1)S(1)} %slice_reduce_fusion.5), channel_id=1, source_target_pairs={{4,0},{8,4},{12,8},{5,1},{9,5},{13,9},{6,2},{10,6},{14,10},{7,3},{... | collective-permute-start | bytes 24584 | tf_op jit(solution)/shard_map/while/body/eval_jaxpr/ppermute | solution.py:10
  45.9 4.4 %collective-permute-start = (bf16[2,2,4,128]{3,2,1,0:T(4,128)(2,1)S(1)}, bf16[2,2,4,128]{3,2,1,0:T(4,128)(2,1)S(1)}, u32[]{:S(2)}, u32[]{:S(2)}) collective-permute-start(bf16[2,2,4,128]{3,2,1,0:T(4,128)(2,1)S(1)} %bitcast.104), channel_id=1, source_target_pairs={{0,16},{4,20},{8,24},{12,28},{16,32},{20,36},{24,40},{28,44},{32,4... | collective-permute-start | bytes 12296 | tf_op jit(solution)/shard_map/while/body/eval_jaxpr/ppermute | solution.py:10
  48.2 4.9 %collective-permute-start.2 = (bf16[2,2,4,128]{3,2,1,0:T(4,128)(2,1)S(1)}, bf16[2,2,4,128]{3,2,1,0:T(4,128)(2,1)S(1)}, u32[]{:S(2)}, u32[]{:S(2)}) collective-permute-start(bf16[2,2,4,128]{3,2,1,0:T(4,128)(2,1)S(1)} %bitcast.105), channel_id=1, source_target_pairs={{16,0},{20,4},{24,8},{28,12},{32,16},{36,20},{40,24},{44,28},{48,3... | collective-permute-start | bytes 12296 | tf_op jit(solution)/shard_map/while/body/eval_jaxpr/ppermute | solution.py:10
  57.4 5.3 %copy-start.3 = (bf16[2,2,4,128,256]{4,3,2,1,0:T(8,128)(2,1)S(1)}, bf16[2,2,4,128,256]{4,3,2,1,0:T(8,128)(2,1)}, u32[]{:S(2)}) copy-start(bf16[2,2,4,128,256]{4,3,2,1,0:T(8,128)(2,1)} %get-tuple-element.571) | copy-start | bytes 3145732 | tf_op jit(solution)/shard_map/while
  57.6 5.6 %copy-start = (bf16[2,2,4,128,256]{3,4,2,1,0:T(8,128)(2,1)}, bf16[2,2,4,128,256]{3,4,2,1,0:T(8,128)(2,1)S(1)}, u32[]{:S(2)}) copy-start(bf16[2,2,4,128,256]{3,4,2,1,0:T(8,128)(2,1)S(1)} %maximum_select_fusion.4) | copy-start | bytes 3145732 | tf_op jit(solution)/shard_map/while
  58.3 19.2 %collective-permute-start.1 = (bf16[2,2,4,256]{3,2,1,0:T(4,128)(2,1)S(1)}, bf16[2,2,4,256]{3,2,1,0:T(4,128)(2,1)S(1)}, u32[]{:S(2)}, u32[]{:S(2)}) collective-permute-start(bf16[2,2,4,256]{3,2,1,0:T(4,128)(2,1)S(1)} %slice_reduce_fusion.4), channel_id=1, source_target_pairs={{0,4},{4,8},{8,12},{1,5},{5,9},{9,13},{2,6},{6,10},{10,14},{3,7},{... | collective-permute-start | bytes 24584 | tf_op jit(solution)/shard_map/while/body/eval_jaxpr/ppermute | solution.py:10
  69.0 8.5 %collective-permute-start.3 = (bf16[2,2,4,256]{3,2,1,0:T(4,128)(2,1)S(1)}, bf16[2,2,4,256]{3,2,1,0:T(4,128)(2,1)S(1)}, u32[]{:S(2)}, u32[]{:S(2)}) collective-permute-start(bf16[2,2,4,256]{3,2,1,0:T(4,128)(2,1)S(1)} %slice_reduce_fusion.5), channel_id=1, source_target_pairs={{4,0},{8,4},{12,8},{5,1},{9,5},{13,9},{6,2},{10,6},{14,10},{7,3},{... | collective-permute-start | bytes 24584 | tf_op jit(solution)/shard_map/while/body/eval_jaxpr/ppermute | solution.py:10
  70.3 4.4 %collective-permute-start = (bf16[2,2,4,128]{3,2,1,0:T(4,128)(2,1)S(1)}, bf16[2,2,4,128]{3,2,1,0:T(4,128)(2,1)S(1)}, u32[]{:S(2)}, u32[]{:S(2)}) collective-permute-start(bf16[2,2,4,128]{3,2,1,0:T(4,128)(2,1)S(1)} %bitcast.104), channel_id=1, source_target_pairs={{0,16},{4,20},{8,24},{12,28},{16,32},{20,36},{24,40},{28,44},{32,4... | collective-permute-start | bytes 12296 | tf_op jit(solution)/shard_map/while/body/eval_jaxpr/ppermute | solution.py:10
  72.6 4.9 %collective-permute-start.2 = (bf16[2,2,4,128]{3,2,1,0:T(4,128)(2,1)S(1)}, bf16[2,2,4,128]{3,2,1,0:T(4,128)(2,1)S(1)}, u32[]{:S(2)}, u32[]{:S(2)}) collective-permute-start(bf16[2,2,4,128]{3,2,1,0:T(4,128)(2,1)S(1)} %bitcast.105), channel_id=1, source_target_pairs={{16,0},{20,4},{24,8},{28,12},{32,16},{36,20},{40,24},{44,28},{48,3... | collective-permute-start | bytes 12296 | tf_op jit(solution)/shard_map/while/body/eval_jaxpr/ppermute | solution.py:10
  81.7 5.3 %copy-start.3 = (bf16[2,2,4,128,256]{4,3,2,1,0:T(8,128)(2,1)S(1)}, bf16[2,2,4,128,256]{4,3,2,1,0:T(8,128)(2,1)}, u32[]{:S(2)}) copy-start(bf16[2,2,4,128,256]{4,3,2,1,0:T(8,128)(2,1)} %get-tuple-element.571) | copy-start | bytes 3145732 | tf_op jit(solution)/shard_map/while
  82.0 5.6 %copy-start = (bf16[2,2,4,128,256]{3,4,2,1,0:T(8,128)(2,1)}, bf16[2,2,4,128,256]{3,4,2,1,0:T(8,128)(2,1)S(1)}, u32[]{:S(2)}) copy-start(bf16[2,2,4,128,256]{3,4,2,1,0:T(8,128)(2,1)S(1)} %maximum_select_fusion.4) | copy-start | bytes 3145732 | tf_op jit(solution)/shard_map/while
  82.7 19.2 %collective-permute-start.1 = (bf16[2,2,4,256]{3,2,1,0:T(4,128)(2,1)S(1)}, bf16[2,2,4,256]{3,2,1,0:T(4,128)(2,1)S(1)}, u32[]{:S(2)}, u32[]{:S(2)}) collective-permute-start(bf16[2,2,4,256]{3,2,1,0:T(4,128)(2,1)S(1)} %slice_reduce_fusion.4), channel_id=1, source_target_pairs={{0,4},{4,8},{8,12},{1,5},{5,9},{9,13},{2,6},{6,10},{10,14},{3,7},{... | collective-permute-start | bytes 24584 | tf_op jit(solution)/shard_map/while/body/eval_jaxpr/ppermute | solution.py:10
  93.3 8.5 %collective-permute-start.3 = (bf16[2,2,4,256]{3,2,1,0:T(4,128)(2,1)S(1)}, bf16[2,2,4,256]{3,2,1,0:T(4,128)(2,1)S(1)}, u32[]{:S(2)}, u32[]{:S(2)}) collective-permute-start(bf16[2,2,4,256]{3,2,1,0:T(4,128)(2,1)S(1)} %slice_reduce_fusion.5), channel_id=1, source_target_pairs={{4,0},{8,4},{12,8},{5,1},{9,5},{13,9},{6,2},{10,6},{14,10},{7,3},{... | collective-permute-start | bytes 24584 | tf_op jit(solution)/shard_map/while/body/eval_jaxpr/ppermute | solution.py:10
  94.7 4.4 %collective-permute-start = (bf16[2,2,4,128]{3,2,1,0:T(4,128)(2,1)S(1)}, bf16[2,2,4,128]{3,2,1,0:T(4,128)(2,1)S(1)}, u32[]{:S(2)}, u32[]{:S(2)}) collective-permute-start(bf16[2,2,4,128]{3,2,1,0:T(4,128)(2,1)S(1)} %bitcast.104), channel_id=1, source_target_pairs={{0,16},{4,20},{8,24},{12,28},{16,32},{20,36},{24,40},{28,44},{32,4... | collective-permute-start | bytes 12296 | tf_op jit(solution)/shard_map/while/body/eval_jaxpr/ppermute | solution.py:10
  96.9 4.9 %collective-permute-start.2 = (bf16[2,2,4,128]{3,2,1,0:T(4,128)(2,1)S(1)}, bf16[2,2,4,128]{3,2,1,0:T(4,128)(2,1)S(1)}, u32[]{:S(2)}, u32[]{:S(2)}) collective-permute-start(bf16[2,2,4,128]{3,2,1,0:T(4,128)(2,1)S(1)} %bitcast.105), channel_id=1, source_target_pairs={{16,0},{20,4},{24,8},{28,12},{32,16},{36,20},{40,24},{44,28},{48,3... | collective-permute-start | bytes 12296 | tf_op jit(solution)/shard_map/while/body/eval_jaxpr/ppermute | solution.py:10
  106.1 5.3 %copy-start.3 = (bf16[2,2,4,128,256]{4,3,2,1,0:T(8,128)(2,1)S(1)}, bf16[2,2,4,128,256]{4,3,2,1,0:T(8,128)(2,1)}, u32[]{:S(2)}) copy-start(bf16[2,2,4,128,256]{4,3,2,1,0:T(8,128)(2,1)} %get-tuple-element.571) | copy-start | bytes 3145732 | tf_op jit(solution)/shard_map/while
  106.3 5.6 %copy-start = (bf16[2,2,4,128,256]{3,4,2,1,0:T(8,128)(2,1)}, bf16[2,2,4,128,256]{3,4,2,1,0:T(8,128)(2,1)S(1)}, u32[]{:S(2)}) copy-start(bf16[2,2,4,128,256]{3,4,2,1,0:T(8,128)(2,1)S(1)} %maximum_select_fusion.4) | copy-start | bytes 3145732 | tf_op jit(solution)/shard_map/while
  107.1 19.2 %collective-permute-start.1 = (bf16[2,2,4,256]{3,2,1,0:T(4,128)(2,1)S(1)}, bf16[2,2,4,256]{3,2,1,0:T(4,128)(2,1)S(1)}, u32[]{:S(2)}, u32[]{:S(2)}) collective-permute-start(bf16[2,2,4,256]{3,2,1,0:T(4,128)(2,1)S(1)} %slice_reduce_fusion.4), channel_id=1, source_target_pairs={{0,4},{4,8},{8,12},{1,5},{5,9},{9,13},{2,6},{6,10},{10,14},{3,7},{... | collective-permute-start | bytes 24584 | tf_op jit(solution)/shard_map/while/body/eval_jaxpr/ppermute | solution.py:10
  117.7 8.5 %collective-permute-start.3 = (bf16[2,2,4,256]{3,2,1,0:T(4,128)(2,1)S(1)}, bf16[2,2,4,256]{3,2,1,0:T(4,128)(2,1)S(1)}, u32[]{:S(2)}, u32[]{:S(2)}) collective-permute-start(bf16[2,2,4,256]{3,2,1,0:T(4,128)(2,1)S(1)} %slice_reduce_fusion.5), channel_id=1, source_target_pairs={{4,0},{8,4},{12,8},{5,1},{9,5},{13,9},{6,2},{10,6},{14,10},{7,3},{... | collective-permute-start | bytes 24584 | tf_op jit(solution)/shard_map/while/body/eval_jaxpr/ppermute | solution.py:10
  119.0 4.4 %collective-permute-start = (bf16[2,2,4,128]{3,2,1,0:T(4,128)(2,1)S(1)}, bf16[2,2,4,128]{3,2,1,0:T(4,128)(2,1)S(1)}, u32[]{:S(2)}, u32[]{:S(2)}) collective-permute-start(bf16[2,2,4,128]{3,2,1,0:T(4,128)(2,1)S(1)} %bitcast.104), channel_id=1, source_target_pairs={{0,16},{4,20},{8,24},{12,28},{16,32},{20,36},{24,40},{28,44},{32,4... | collective-permute-start | bytes 12296 | tf_op jit(solution)/shard_map/while/body/eval_jaxpr/ppermute | solution.py:10
  121.3 4.9 %collective-permute-start.2 = (bf16[2,2,4,128]{3,2,1,0:T(4,128)(2,1)S(1)}, bf16[2,2,4,128]{3,2,1,0:T(4,128)(2,1)S(1)}, u32[]{:S(2)}, u32[]{:S(2)}) collective-permute-start(bf16[2,2,4,128]{3,2,1,0:T(4,128)(2,1)S(1)} %bitcast.105), channel_id=1, source_target_pairs={{16,0},{20,4},{24,8},{28,12},{32,16},{36,20},{40,24},{44,28},{48,3... | collective-permute-start | bytes 12296 | tf_op jit(solution)/shard_map/while/body/eval_jaxpr/ppermute | solution.py:10
  130.5 5.3 %copy-start.3 = (bf16[2,2,4,128,256]{4,3,2,1,0:T(8,128)(2,1)S(1)}, bf16[2,2,4,128,256]{4,3,2,1,0:T(8,128)(2,1)}, u32[]{:S(2)}) copy-start(bf16[2,2,4,128,256]{4,3,2,1,0:T(8,128)(2,1)} %get-tuple-element.571) | copy-start | bytes 3145732 | tf_op jit(solution)/shard_map/while
  130.7 5.6 %copy-start = (bf16[2,2,4,128,256]{3,4,2,1,0:T(8,128)(2,1)}, bf16[2,2,4,128,256]{3,4,2,1,0:T(8,128)(2,1)S(1)}, u32[]{:S(2)}) copy-start(bf16[2,2,4,128,256]{3,4,2,1,0:T(8,128)(2,1)S(1)} %maximum_select_fusion.4) | copy-start | bytes 3145732 | tf_op jit(solution)/shard_map/while
  131.4 19.2 %collective-permute-start.1 = (bf16[2,2,4,256]{3,2,1,0:T(4,128)(2,1)S(1)}, bf16[2,2,4,256]{3,2,1,0:T(4,128)(2,1)S(1)}, u32[]{:S(2)}, u32[]{:S(2)}) collective-permute-start(bf16[2,2,4,256]{3,2,1,0:T(4,128)(2,1)S(1)} %slice_reduce_fusion.4), channel_id=1, source_target_pairs={{0,4},{4,8},{8,12},{1,5},{5,9},{9,13},{2,6},{6,10},{10,14},{3,7},{... | collective-permute-start | bytes 24584 | tf_op jit(solution)/shard_map/while/body/eval_jaxpr/ppermute | solution.py:10
  142.1 8.5 %collective-permute-start.3 = (bf16[2,2,4,256]{3,2,1,0:T(4,128)(2,1)S(1)}, bf16[2,2,4,256]{3,2,1,0:T(4,128)(2,1)S(1)}, u32[]{:S(2)}, u32[]{:S(2)}) collective-permute-start(bf16[2,2,4,256]{3,2,1,0:T(4,128)(2,1)S(1)} %slice_reduce_fusion.5), channel_id=1, source_target_pairs={{4,0},{8,4},{12,8},{5,1},{9,5},{13,9},{6,2},{10,6},{14,10},{7,3},{... | collective-permute-start | bytes 24584 | tf_op jit(solution)/shard_map/while/body/eval_jaxpr/ppermute | solution.py:10
  143.4 4.4 %collective-permute-start = (bf16[2,2,4,128]{3,2,1,0:T(4,128)(2,1)S(1)}, bf16[2,2,4,128]{3,2,1,0:T(4,128)(2,1)S(1)}, u32[]{:S(2)}, u32[]{:S(2)}) collective-permute-start(bf16[2,2,4,128]{3,2,1,0:T(4,128)(2,1)S(1)} %bitcast.104), channel_id=1, source_target_pairs={{0,16},{4,20},{8,24},{12,28},{16,32},{20,36},{24,40},{28,44},{32,4... | collective-permute-start | bytes 12296 | tf_op jit(solution)/shard_map/while/body/eval_jaxpr/ppermute | solution.py:10
  145.7 4.9 %collective-permute-start.2 = (bf16[2,2,4,128]{3,2,1,0:T(4,128)(2,1)S(1)}, bf16[2,2,4,128]{3,2,1,0:T(4,128)(2,1)S(1)}, u32[]{:S(2)}, u32[]{:S(2)}) collective-permute-start(bf16[2,2,4,128]{3,2,1,0:T(4,128)(2,1)S(1)} %bitcast.105), channel_id=1, source_target_pairs={{16,0},{20,4},{24,8},{28,12},{32,16},{36,20},{40,24},{44,28},{48,3... | collective-permute-start | bytes 12296 | tf_op jit(solution)/shard_map/while/body/eval_jaxpr/ppermute | solution.py:10
  154.8 5.3 %copy-start.3 = (bf16[2,2,4,128,256]{4,3,2,1,0:T(8,128)(2,1)S(1)}, bf16[2,2,4,128,256]{4,3,2,1,0:T(8,128)(2,1)}, u32[]{:S(2)}) copy-start(bf16[2,2,4,128,256]{4,3,2,1,0:T(8,128)(2,1)} %get-tuple-element.571) | copy-start | bytes 3145732 | tf_op jit(solution)/shard_map/while
  155.0 5.6 %copy-start = (bf16[2,2,4,128,256]{3,4,2,1,0:T(8,128)(2,1)}, bf16[2,2,4,128,256]{3,4,2,1,0:T(8,128)(2,1)S(1)}, u32[]{:S(2)}) copy-start(bf16[2,2,4,128,256]{3,4,2,1,0:T(8,128)(2,1)S(1)} %maximum_select_fusion.4) | copy-start | bytes 3145732 | tf_op jit(solution)/shard_map/while
  155.8 19.2 %collective-permute-start.1 = (bf16[2,2,4,256]{3,2,1,0:T(4,128)(2,1)S(1)}, bf16[2,2,4,256]{3,2,1,0:T(4,128)(2,1)S(1)}, u32[]{:S(2)}, u32[]{:S(2)}) collective-permute-start(bf16[2,2,4,256]{3,2,1,0:T(4,128)(2,1)S(1)} %slice_reduce_fusion.4), channel_id=1, source_target_pairs={{0,4},{4,8},{8,12},{1,5},{5,9},{9,13},{2,6},{6,10},{10,14},{3,7},{... | collective-permute-start | bytes 24584 | tf_op jit(solution)/shard_map/while/body/eval_jaxpr/ppermute | solution.py:10
  166.4 8.5 %collective-permute-start.3 = (bf16[2,2,4,256]{3,2,1,0:T(4,128)(2,1)S(1)}, bf16[2,2,4,256]{3,2,1,0:T(4,128)(2,1)S(1)}, u32[]{:S(2)}, u32[]{:S(2)}) collective-permute-start(bf16[2,2,4,256]{3,2,1,0:T(4,128)(2,1)S(1)} %slice_reduce_fusion.5), channel_id=1, source_target_pairs={{4,0},{8,4},{12,8},{5,1},{9,5},{13,9},{6,2},{10,6},{14,10},{7,3},{... | collective-permute-start | bytes 24584 | tf_op jit(solution)/shard_map/while/body/eval_jaxpr/ppermute | solution.py:10
  167.8 4.4 %collective-permute-start = (bf16[2,2,4,128]{3,2,1,0:T(4,128)(2,1)S(1)}, bf16[2,2,4,128]{3,2,1,0:T(4,128)(2,1)S(1)}, u32[]{:S(2)}, u32[]{:S(2)}) collective-permute-start(bf16[2,2,4,128]{3,2,1,0:T(4,128)(2,1)S(1)} %bitcast.104), channel_id=1, source_target_pairs={{0,16},{4,20},{8,24},{12,28},{16,32},{20,36},{24,40},{28,44},{32,4... | collective-permute-start | bytes 12296 | tf_op jit(solution)/shard_map/while/body/eval_jaxpr/ppermute | solution.py:10
  170.0 4.9 %collective-permute-start.2 = (bf16[2,2,4,128]{3,2,1,0:T(4,128)(2,1)S(1)}, bf16[2,2,4,128]{3,2,1,0:T(4,128)(2,1)S(1)}, u32[]{:S(2)}, u32[]{:S(2)}) collective-permute-start(bf16[2,2,4,128]{3,2,1,0:T(4,128)(2,1)S(1)} %bitcast.105), channel_id=1, source_target_pairs={{16,0},{20,4},{24,8},{28,12},{32,16},{36,20},{40,24},{44,28},{48,3... | collective-permute-start | bytes 12296 | tf_op jit(solution)/shard_map/while/body/eval_jaxpr/ppermute | solution.py:10
  179.4 5.6 %copy-start = (bf16[2,2,4,128,256]{3,4,2,1,0:T(8,128)(2,1)}, bf16[2,2,4,128,256]{3,4,2,1,0:T(8,128)(2,1)S(1)}, u32[]{:S(2)}) copy-start(bf16[2,2,4,128,256]{3,4,2,1,0:T(8,128)(2,1)S(1)} %maximum_select_fusion.4) | copy-start | bytes 3145732 | tf_op jit(solution)/shard_map/while
  180.1 19.2 %collective-permute-start.1 = (bf16[2,2,4,256]{3,2,1,0:T(4,128)(2,1)S(1)}, bf16[2,2,4,256]{3,2,1,0:T(4,128)(2,1)S(1)}, u32[]{:S(2)}, u32[]{:S(2)}) collective-permute-start(bf16[2,2,4,256]{3,2,1,0:T(4,128)(2,1)S(1)} %slice_reduce_fusion.4), channel_id=1, source_target_pairs={{0,4},{4,8},{8,12},{1,5},{5,9},{9,13},{2,6},{6,10},{10,14},{3,7},{... | collective-permute-start | bytes 24584 | tf_op jit(solution)/shard_map/while/body/eval_jaxpr/ppermute | solution.py:10
  190.8 8.5 %collective-permute-start.3 = (bf16[2,2,4,256]{3,2,1,0:T(4,128)(2,1)S(1)}, bf16[2,2,4,256]{3,2,1,0:T(4,128)(2,1)S(1)}, u32[]{:S(2)}, u32[]{:S(2)}) collective-permute-start(bf16[2,2,4,256]{3,2,1,0:T(4,128)(2,1)S(1)} %slice_reduce_fusion.5), channel_id=1, source_target_pairs={{4,0},{8,4},{12,8},{5,1},{9,5},{13,9},{6,2},{10,6},{14,10},{7,3},{... | collective-permute-start | bytes 24584 | tf_op jit(solution)/shard_map/while/body/eval_jaxpr/ppermute | solution.py:10
  192.1 4.4 %collective-permute-start = (bf16[2,2,4,128]{3,2,1,0:T(4,128)(2,1)S(1)}, bf16[2,2,4,128]{3,2,1,0:T(4,128)(2,1)S(1)}, u32[]{:S(2)}, u32[]{:S(2)}) collective-permute-start(bf16[2,2,4,128]{3,2,1,0:T(4,128)(2,1)S(1)} %bitcast.104), channel_id=1, source_target_pairs={{0,16},{4,20},{8,24},{12,28},{16,32},{20,36},{24,40},{28,44},{32,4... | collective-permute-start | bytes 12296 | tf_op jit(solution)/shard_map/while/body/eval_jaxpr/ppermute | solution.py:10
  194.4 4.9 %collective-permute-start.2 = (bf16[2,2,4,128]{3,2,1,0:T(4,128)(2,1)S(1)}, bf16[2,2,4,128]{3,2,1,0:T(4,128)(2,1)S(1)}, u32[]{:S(2)}, u32[]{:S(2)}) collective-permute-start(bf16[2,2,4,128]{3,2,1,0:T(4,128)(2,1)S(1)} %bitcast.105), channel_id=1, source_target_pairs={{16,0},{20,4},{24,8},{28,12},{32,16},{36,20},{40,24},{44,28},{48,3... | collective-permute-start | bytes 12296 | tf_op jit(solution)/shard_map/while/body/eval_jaxpr/ppermute | solution.py:10
  203.8 5.6 %copy-start = (bf16[2,2,4,128,256]{3,4,2,1,0:T(8,128)(2,1)}, bf16[2,2,4,128,256]{3,4,2,1,0:T(8,128)(2,1)S(1)}, u32[]{:S(2)}) copy-start(bf16[2,2,4,128,256]{3,4,2,1,0:T(8,128)(2,1)S(1)} %maximum_select_fusion.4) | copy-start | bytes 3145732 | tf_op jit(solution)/shard_map/while
  204.5 19.2 %collective-permute-start.1 = (bf16[2,2,4,256]{3,2,1,0:T(4,128)(2,1)S(1)}, bf16[2,2,4,256]{3,2,1,0:T(4,128)(2,1)S(1)}, u32[]{:S(2)}, u32[]{:S(2)}) collective-permute-start(bf16[2,2,4,256]{3,2,1,0:T(4,128)(2,1)S(1)} %slice_reduce_fusion.4), channel_id=1, source_target_pairs={{0,4},{4,8},{8,12},{1,5},{5,9},{9,13},{2,6},{6,10},{10,14},{3,7},{... | collective-permute-start | bytes 24584 | tf_op jit(solution)/shard_map/while/body/eval_jaxpr/ppermute | solution.py:10
  215.1 8.5 %collective-permute-start.3 = (bf16[2,2,4,256]{3,2,1,0:T(4,128)(2,1)S(1)}, bf16[2,2,4,256]{3,2,1,0:T(4,128)(2,1)S(1)}, u32[]{:S(2)}, u32[]{:S(2)}) collective-permute-start(bf16[2,2,4,256]{3,2,1,0:T(4,128)(2,1)S(1)} %slice_reduce_fusion.5), channel_id=1, source_target_pairs={{4,0},{8,4},{12,8},{5,1},{9,5},{13,9},{6,2},{10,6},{14,10},{7,3},{... | collective-permute-start | bytes 24584 | tf_op jit(solution)/shard_map/while/body/eval_jaxpr/ppermute | solution.py:10
  216.5 4.4 %collective-permute-start = (bf16[2,2,4,128]{3,2,1,0:T(4,128)(2,1)S(1)}, bf16[2,2,4,128]{3,2,1,0:T(4,128)(2,1)S(1)}, u32[]{:S(2)}, u32[]{:S(2)}) collective-permute-start(bf16[2,2,4,128]{3,2,1,0:T(4,128)(2,1)S(1)} %bitcast.104), channel_id=1, source_target_pairs={{0,16},{4,20},{8,24},{12,28},{16,32},{20,36},{24,40},{28,44},{32,4... | collective-permute-start | bytes 12296 | tf_op jit(solution)/shard_map/while/body/eval_jaxpr/ppermute | solution.py:10
  218.8 4.9 %collective-permute-start.2 = (bf16[2,2,4,128]{3,2,1,0:T(4,128)(2,1)S(1)}, bf16[2,2,4,128]{3,2,1,0:T(4,128)(2,1)S(1)}, u32[]{:S(2)}, u32[]{:S(2)}) collective-permute-start(bf16[2,2,4,128]{3,2,1,0:T(4,128)(2,1)S(1)} %bitcast.105), channel_id=1, source_target_pairs={{16,0},{20,4},{24,8},{28,12},{32,16},{36,20},{40,24},{44,28},{48,3... | collective-permute-start | bytes 12296 | tf_op jit(solution)/shard_map/while/body/eval_jaxpr/ppermute | solution.py:10
  228.1 5.6 %copy-start = (bf16[2,2,4,128,256]{3,4,2,1,0:T(8,128)(2,1)}, bf16[2,2,4,128,256]{3,4,2,1,0:T(8,128)(2,1)S(1)}, u32[]{:S(2)}) copy-start(bf16[2,2,4,128,256]{3,4,2,1,0:T(8,128)(2,1)S(1)} %maximum_select_fusion.4) | copy-start | bytes 3145732 | tf_op jit(solution)/shard_map/while
  228.9 19.2 %collective-permute-start.1 = (bf16[2,2,4,256]{3,2,1,0:T(4,128)(2,1)S(1)}, bf16[2,2,4,256]{3,2,1,0:T(4,128)(2,1)S(1)}, u32[]{:S(2)}, u32[]{:S(2)}) collective-permute-start(bf16[2,2,4,256]{3,2,1,0:T(4,128)(2,1)S(1)} %slice_reduce_fusion.4), channel_id=1, source_target_pairs={{0,4},{4,8},{8,12},{1,5},{5,9},{9,13},{2,6},{6,10},{10,14},{3,7},{... | collective-permute-start | bytes 24584 | tf_op jit(solution)/shard_map/while/body/eval_jaxpr/ppermute | solution.py:10
  239.5 8.5 %collective-permute-start.3 = (bf16[2,2,4,256]{3,2,1,0:T(4,128)(2,1)S(1)}, bf16[2,2,4,256]{3,2,1,0:T(4,128)(2,1)S(1)}, u32[]{:S(2)}, u32[]{:S(2)}) collective-permute-start(bf16[2,2,4,256]{3,2,1,0:T(4,128)(2,1)S(1)} %slice_reduce_fusion.5), channel_id=1, source_target_pairs={{4,0},{8,4},{12,8},{5,1},{9,5},{13,9},{6,2},{10,6},{14,10},{7,3},{... | collective-permute-start | bytes 24584 | tf_op jit(solution)/shard_map/while/body/eval_jaxpr/ppermute | solution.py:10
  240.8 4.4 %collective-permute-start = (bf16[2,2,4,128]{3,2,1,0:T(4,128)(2,1)S(1)}, bf16[2,2,4,128]{3,2,1,0:T(4,128)(2,1)S(1)}, u32[]{:S(2)}, u32[]{:S(2)}) collective-permute-start(bf16[2,2,4,128]{3,2,1,0:T(4,128)(2,1)S(1)} %bitcast.104), channel_id=1, source_target_pairs={{0,16},{4,20},{8,24},{12,28},{16,32},{20,36},{24,40},{28,44},{32,4... | collective-permute-start | bytes 12296 | tf_op jit(solution)/shard_map/while/body/eval_jaxpr/ppermute | solution.py:10
  243.1 4.9 %collective-permute-start.2 = (bf16[2,2,4,128]{3,2,1,0:T(4,128)(2,1)S(1)}, bf16[2,2,4,128]{3,2,1,0:T(4,128)(2,1)S(1)}, u32[]{:S(2)}, u32[]{:S(2)}) collective-permute-start(bf16[2,2,4,128]{3,2,1,0:T(4,128)(2,1)S(1)} %bitcast.105), channel_id=1, source_target_pairs={{16,0},{20,4},{24,8},{28,12},{32,16},{36,20},{40,24},{44,28},{48,3... | collective-permute-start | bytes 12296 | tf_op jit(solution)/shard_map/while/body/eval_jaxpr/ppermute | solution.py:10
  252.5 5.6 %copy-start = (bf16[2,2,4,128,256]{3,4,2,1,0:T(8,128)(2,1)}, bf16[2,2,4,128,256]{3,4,2,1,0:T(8,128)(2,1)S(1)}, u32[]{:S(2)}) copy-start(bf16[2,2,4,128,256]{3,4,2,1,0:T(8,128)(2,1)S(1)} %maximum_select_fusion.4) | copy-start | bytes 3145732 | tf_op jit(solution)/shard_map/while
  253.2 19.2 %collective-permute-start.1 = (bf16[2,2,4,256]{3,2,1,0:T(4,128)(2,1)S(1)}, bf16[2,2,4,256]{3,2,1,0:T(4,128)(2,1)S(1)}, u32[]{:S(2)}, u32[]{:S(2)}) collective-permute-start(bf16[2,2,4,256]{3,2,1,0:T(4,128)(2,1)S(1)} %slice_reduce_fusion.4), channel_id=1, source_target_pairs={{0,4},{4,8},{8,12},{1,5},{5,9},{9,13},{2,6},{6,10},{10,14},{3,7},{... | collective-permute-start | bytes 24584 | tf_op jit(solution)/shard_map/while/body/eval_jaxpr/ppermute | solution.py:10
  263.9 8.5 %collective-permute-start.3 = (bf16[2,2,4,256]{3,2,1,0:T(4,128)(2,1)S(1)}, bf16[2,2,4,256]{3,2,1,0:T(4,128)(2,1)S(1)}, u32[]{:S(2)}, u32[]{:S(2)}) collective-permute-start(bf16[2,2,4,256]{3,2,1,0:T(4,128)(2,1)S(1)} %slice_reduce_fusion.5), channel_id=1, source_target_pairs={{4,0},{8,4},{12,8},{5,1},{9,5},{13,9},{6,2},{10,6},{14,10},{7,3},{... | collective-permute-start | bytes 24584 | tf_op jit(solution)/shard_map/while/body/eval_jaxpr/ppermute | solution.py:10
  265.2 4.4 %collective-permute-start = (bf16[2,2,4,128]{3,2,1,0:T(4,128)(2,1)S(1)}, bf16[2,2,4,128]{3,2,1,0:T(4,128)(2,1)S(1)}, u32[]{:S(2)}, u32[]{:S(2)}) collective-permute-start(bf16[2,2,4,128]{3,2,1,0:T(4,128)(2,1)S(1)} %bitcast.104), channel_id=1, source_target_pairs={{0,16},{4,20},{8,24},{12,28},{16,32},{20,36},{24,40},{28,44},{32,4... | collective-permute-start | bytes 12296 | tf_op jit(solution)/shard_map/while/body/eval_jaxpr/ppermute | solution.py:10
  267.5 4.9 %collective-permute-start.2 = (bf16[2,2,4,128]{3,2,1,0:T(4,128)(2,1)S(1)}, bf16[2,2,4,128]{3,2,1,0:T(4,128)(2,1)S(1)}, u32[]{:S(2)}, u32[]{:S(2)}) collective-permute-start(bf16[2,2,4,128]{3,2,1,0:T(4,128)(2,1)S(1)} %bitcast.105), channel_id=1, source_target_pairs={{16,0},{20,4},{24,8},{28,12},{32,16},{36,20},{40,24},{44,28},{48,3... | collective-permute-start | bytes 12296 | tf_op jit(solution)/shard_map/while/body/eval_jaxpr/ppermute | solution.py:10
  273.6 13.6 %collective-permute-start.4 = (bf16[2,2,2,1,128,256]{5,4,3,2,1,0:T(8,128)(2,1)S(1)}, bf16[2,2,2,1,128,256]{5,4,3,2,1,0:T(8,128)(2,1)S(1)}, u32[]{:S(2)}, u32[]{:S(2)}) collective-permute-start(bf16[2,2,2,1,128,256]{5,4,3,2,1,0:T(8,128)(2,1)S(1)} %get-tuple-element.410), channel_id=1, source_target_pairs={{0,1},{1,2},{2,3},{4,5},{5,6},{6,7},{8,9},{9,10},{10,11},{12,13},{... | collective-permute-start | bytes 1572872 | tf_op jit(solution)/shard_map/ppermute | solution.py:21
  276.7 14.6 %collective-permute-start.5 = (bf16[2,2,2,1,128,256]{5,4,3,2,1,0:T(8,128)(2,1)S(1)}, bf16[2,2,2,1,128,256]{5,4,3,2,1,0:T(8,128)(2,1)S(1)}, u32[]{:S(2)}, u32[]{:S(2)}) collective-permute-start(bf16[2,2,2,1,128,256]{5,4,3,2,1,0:T(8,128)(2,1)S(1)} %get-tuple-element.411), channel_id=1, source_target_pairs={{1,0},{2,1},{3,2},{5,4},{6,5},{7,6},{9,8},{10,9},{11,10},{13,12},{... | collective-permute-start | bytes 1572872 | tf_op jit(solution)/shard_map/ppermute | solution.py:23
  (26 other events, 63.1 us)
where the time goes:
time: 298 us; the launch traced here: 296 us
  starting transfers between devices  115 us (39%)
  matrix products  75.2 us (25%)
  waiting for transfers between devices  44.5 us (15%)
  other arithmetic  41.9 us (14%)
  local copies, waits for them, and re-layouts  15.4 us (5%)
  loops' own time  3 us (1%)
    ppermute x44, starting transfers between devices, passed_along(): lax.ppermute(value, axis, [(source, source + steps) for source in range(l...  110 us
    another operation x44, other arithmetic  32.6 us
    ppermute x44, waiting for transfers between devices, passed_along(): lax.ppermute(value, axis, [(source, source + steps) for source in range(l...  31.2 us
    dot_general x22, matrix products, solve_along_x(): jnp.einsum(form, field, real_matrix, preferred_element_type=jnp.float32)  27.1 us
    dot_general x22, matrix products, solve_along_y(): jnp.einsum(form, imag_matrix, field, preferred_element_type=jnp.float32)  25.1 us
    dot_general x22, matrix products, solve_along_x(): jnp.einsum(form, field, imag_matrix, preferred_element_type=jnp.float32)  12.7 us
    dot_general x22, matrix products, solve_along_y(): jnp.einsum(form, real_matrix, field, preferred_element_type=jnp.float32)  10.4 us
    ppermute x1, waiting for transfers between devices, extended(): lax.ppermute(tail, axis, [(i, (i + 1) % count) for i in range(ends)])  9.17 us
  transfers between devices with their start and end apart: 46, of which 13 were waited for; matrix products, arithmetic and copies ran while one was open for 23% of the time, Pallas kernels for 0%

commit v1 on v0

v1 whole, which is shorter than its diff:
```python
import functools

import jax
import jax.numpy as jnp
from jax import lax
from jax.experimental import pallas as pl
from jax.experimental.pallas import tpu as pltpu
from jax.sharding import PartitionSpec as P

MESH = pl.DeviceIdType.MESH
BF = jnp.bfloat16
F32 = jnp.float32


def dot(left, right):
    return jnp.dot(left, right, preferred_element_type=F32)


def dot_last(left, right):
    return lax.dot_general(left, right, (((1,), (1,)), ((), ())), preferred_element_type=F32)


def dot_first(left, right):
    return lax.dot_general(left, right, (((0,), (0,)), ((), ())), preferred_element_type=F32)


def kernel(
    sizes, shots, depths, ny, nx,
    s_hbm, a_hbm, x_hbm, y_hbm, so_hbm, ao_hbm, g_hbm,
    src, xraw, yraw, xmat, gmat, ymat, edge, sxv, ysv, ext, ab, plane_out, plane_in,
    c_in, r_in, c_out, r_out, pq, half, base, field, grad,
    load_sem, plane_send, plane_recv, halo_send, halo_recv,
    c_send, c_recv, r_send, r_recv, out_sem, grad_sem,
):
    n_gx, n_gy, n_gz = sizes
    gx, gy, gz = lax.axis_index("gx"), lax.axis_index("gy"), lax.axis_index("gz")
    rhs = shots * depths
    c_in[...] = jnp.zeros_like(c_in)
    r_in[...] = jnp.zeros_like(r_in)
    barrier = pltpu.get_barrier_semaphore()
    for axis, index, count in (("gx", gx, n_gx), ("gy", gy, n_gy), ("gz", gz, n_gz)):
        @pl.when(index > 0)
        def _():
            pl.semaphore_signal(barrier, inc=1, device_id={axis: index - 1}, device_id_type=MESH)

        @pl.when(index < count - 1)
        def _():
            pl.semaphore_signal(barrier, inc=1, device_id={axis: index + 1}, device_id_type=MESH)

    loads = [
        pltpu.make_async_copy(x_hbm.at[0, 0], xraw, load_sem.at[0]),
        pltpu.make_async_copy(y_hbm.at[0, 0], yraw, load_sem.at[1]),
        pltpu.make_async_copy(s_hbm, src.at[0, :, :, pl.ds(1, depths)], load_sem.at[2]),
        pltpu.make_async_copy(a_hbm, src.at[1, :, :, pl.ds(1, depths)], load_sem.at[3]),
    ]
    for load in loads:
        load.start()

    @pl.when(gz == 0)
    def _():
        plane_in[:, 0] = jnp.zeros_like(plane_in[:, 0])
        src[:, :, :, 0] = jnp.zeros_like(src[:, :, :, 0])

    @pl.when(gz == n_gz - 1)
    def _():
        plane_in[:, 1] = jnp.zeros_like(plane_in[:, 1])
        src[:, :, :, depths + 1] = jnp.zeros_like(src[:, :, :, depths + 1])

    loads[0].wait()
    loads[1].wait()
    for way in range(2):
        xr, xi, yr, yi = xraw[0], xraw[1], yraw[0], yraw[1]
        xrt, xit, yrt, yit = xr.T, xi.T, yr.T, yi.T
        mr, mi = (xrt, xit) if way == 0 else (xr, xi)
        gr, gi = (yrt, yit) if way == 0 else (yr, yi)
        lr, li = (yr, yi) if way == 0 else (yrt, yit)
        xmat[way, :nx, :nx] = mr
        xmat[way, :nx, nx:] = mi
        xmat[way, nx:, :nx] = -mi
        xmat[way, nx:, nx:] = mr
        gmat[way, :ny, :ny] = gr
        gmat[way, :ny, ny:] = gi
        gmat[way, ny:, :ny] = -gi
        gmat[way, ny:, ny:] = gr
        ymat[way, :ny, :ny] = lr
        ymat[way, :ny, ny:] = -li
        ymat[way, ny:, :ny] = li
        ymat[way, ny:, ny:] = lr
        x_row = 0 if way == 0 else nx - 1
        y_row = 0 if way == 0 else ny - 1
        xe = jnp.concatenate([mr[x_row:x_row + 1], mi[x_row:x_row + 1]], axis=1).astype(F32)
        ye = jnp.concatenate([gr[y_row:y_row + 1], gi[y_row:y_row + 1]], axis=1).astype(F32)
        edge[way, 0:1, : 2 * ny] = ye
        edge[way, 0:1, 2 * ny:] = xe

    loads[2].wait()
    loads[3].wait()

    def pair_rows(real, imag):
        rows = lax.broadcasted_iota(jnp.int32, (8, 1), 0)
        first = jnp.where(rows == 0, real, jnp.where(rows == 1, imag, 0.0))
        second = jnp.where(rows == 0, -imag, jnp.where(rows == 1, real, 0.0))
        return first.astype(BF), second.astype(BF)

    def plane_copies(way):
        down = pltpu.make_async_remote_copy(
            src_ref=plane_out.at[way, 0], dst_ref=plane_in.at[way, 1],
            send_sem=plane_send.at[way, 0], recv_sem=plane_recv.at[way, 1],
            device_id={"gz": gz - 1}, device_id_type=MESH,
        )
        up = pltpu.make_async_remote_copy(
            src_ref=plane_out.at[way, 1], dst_ref=plane_in.at[way, 0],
            send_sem=plane_send.at[way, 1], recv_sem=plane_recv.at[way, 0],
            device_id={"gz": gz + 1}, device_id_type=MESH,
        )
        return down, up

    def halo_copies(way):
        down = pltpu.make_async_remote_copy(
            src_ref=src.at[way, :, :, 1], dst_ref=src.at[way, :, :, depths + 1],
            send_sem=halo_send.at[way, 0], recv_sem=halo_recv.at[way, 1],
            device_id={"gz": gz - 1}, device_id_type=MESH,
        )
        up = pltpu.make_async_remote_copy(
            src_ref=src.at[way, :, :, depths], dst_ref=src.at[way, :, :, 0],
            send_sem=halo_send.at[way, 1], recv_sem=halo_recv.at[way, 0],
            device_id={"gz": gz + 1}, device_id_type=MESH,
        )
        return down, up

    def start_both(copies):
        @pl.when(gz > 0)
        def _():
            copies[0].start()

        @pl.when(gz < n_gz - 1)
        def _():
            copies[1].start()

    def wait_arrivals(copies):
        @pl.when(gz > 0)
        def _():
            copies[1].wait_recv()

        @pl.when(gz < n_gz - 1)
        def _():
            copies[0].wait_recv()

    def wait_departures(copies):
        @pl.when(gz > 0)
        def _():
            copies[0].wait_send()

        @pl.when(gz < n_gz - 1)
        def _():
            copies[1].wait_send()

    def local_terms(way):
        other = edge[1 - way, 0:1, :]
        x_first, x_second = pair_rows(other[:, 2 * ny: 2 * ny + nx], other[:, 2 * ny + nx:])
        y_first, y_second = pair_rows(other[:, :ny], other[:, ny: 2 * ny])
        y_both = jnp.concatenate([y_first, y_second], axis=1)
        for s in range(shots):
            for d in range(0, depths, 2):
                real = src[way, s, 0, pl.ds(1 + d, 2)].reshape(2 * ny, nx)
                imag = src[way, s, 1, pl.ds(1 + d, 2)].reshape(2 * ny, nx)
                res = dot_last(x_first, real) + dot_last(x_second, imag)
                for k in range(2):
                    q = (d + k) * shots + s
                    sxv[q:q + 1, :ny] = res[0:1, k * ny:(k + 1) * ny]
                    sxv[q:q + 1, ny:] = res[1:2, k * ny:(k + 1) * ny]
            for d in range(depths):
                both = jnp.concatenate([src[way, s, 0, 1 + d], src[way, s, 1, 1 + d]], axis=0)
                res = dot(y_both, both)
                q = d * shots + s
                ysv[q:q + 1, :nx] = res[0:1]
                ysv[q:q + 1, nx:] = res[1:2]
        col = dot(sxv[...].astype(BF), gmat[way])
        row = dot(ysv[...].astype(BF), xmat[way])
        ab[way, :, : 2 * ny] = col
        ab[way, :, 2 * ny:] = row
        plane_out[way, 0] = ab[way, :shots]
        plane_out[way, 1] = ab[way, rhs - shots:]

    def averaged_terms(way):
        ext[:shots] = plane_in[way, 0]
        ext[shots:shots + rhs] = ab[way]
        ext[shots + rhs:rhs + 2 * shots] = plane_in[way, 1]
        near = ext[:rhs] + ext[2 * shots: 2 * shots + rhs]
        ab[way] = 0.5 * ext[shots:shots + rhs] + 0.25 * near

    def hop_copies(way):
        step = 1 - 2 * way
        col = pltpu.make_async_remote_copy(
            src_ref=c_out.at[way], dst_ref=c_in.at[way],
            send_sem=c_send.at[way], recv_sem=c_recv.at[way],
            device_id={"gx": gx + step}, device_id_type=MESH,
        )
        row = pltpu.make_async_remote_copy(
            src_ref=r_out.at[way], dst_ref=r_in.at[way],
            send_sem=r_send.at[way], recv_sem=r_recv.at[way],
            device_id={"gy": gy + step}, device_id_type=MESH,
        )
        return col, row

    def places(way):
        at_x = gx + way * (n_gx - 1 - 2 * gx)
        at_y = gy + way * (n_gy - 1 - 2 * gy)
        return at_x, at_y

    def hop(way):
        at_x, at_y = places(way)
        send_col, send_row = hop_copies(way)

        @pl.when(at_x > 0)
        def _():
            send_col.wait_recv()

        @pl.when(at_y > 0)
        def _():
            send_row.wait_recv()

        p = dot(c_in[way], gmat[way])
        q = dot(r_in[way], xmat[way])
        pq[way, :, : 2 * ny] = p
        pq[way, :, 2 * ny:] = q
        forward = jnp.broadcast_to(way == 0, (1, 1))

        def out_lane(value):
            n = value.shape[1]
            return jnp.where(forward, value[:, n - 1:], value[:, :1])

        ey, ex = edge[way, 0:1, : 2 * ny], edge[way, 0:1, 2 * ny:]
        eyr, eyi, exr, exi = ey[:, :ny], ey[:, ny:], ex[:, :nx], ex[:, nx:]
        pr, pi, qr, qi = p[:, :ny], p[:, ny:], q[:, :nx], q[:, nx:]
        xr, xi, yr, yi = out_lane(exr), out_lane(exi), out_lane(eyr), out_lane(eyi)
        tr, ti, sr, si = out_lane(pr), out_lane(pi), out_lane(qr), out_lane(qi)
        c_out[way, :, :ny] = (ab[way, :, :ny] + (pr * xr - pi * xi) + (eyr * sr - eyi * si)).astype(BF)
        c_out[way, :, ny:] = (
            ab[way, :, ny: 2 * ny] + (pr * xi + pi * xr) + (eyr * si + eyi * sr)
        ).astype(BF)

        @pl.when(at_x < n_gx - 1)
        def _():
            send_col.start()

        r_out[way, :, :nx] = (
            ab[way, :, 2 * ny: 2 * ny + nx] + (exr * tr - exi * ti) + (qr * yr - qi * yi)
        ).astype(BF)
        r_out[way, :, nx:] = (
            ab[way, :, 2 * ny + nx:] + (exr * ti + exi * tr) + (qr * yi + qi * yr)
        ).astype(BF)

        @pl.when(at_y < n_gy - 1)
        def _():
            send_row.start()

    def hop_departures(way):
        at_x, at_y = places(way)
        send_col, send_row = hop_copies(way)

        @pl.when(at_x < n_gx - 1)
        def _():
            send_col.wait_send()

        @pl.when(at_y < n_gy - 1)
        def _():
            send_row.wait_send()

    def base_fields(way):
        def two_depths(i, carry):
            s, d = i // (depths // 2), (i % (depths // 2)) * 2
            planes = []
            for part in range(2):
                low = src[way, s, part, pl.ds(d, 2)].astype(F32)
                mid = src[way, s, part, pl.ds(d + 1, 2)].astype(F32)
                high = src[way, s, part, pl.ds(d + 2, 2)].astype(F32)
                mean = 0.5 * mid + 0.25 * (low + high)
                planes.append(mean.astype(BF).reshape(2 * ny, nx))
            out = dot(jnp.concatenate(planes, axis=1), xmat[way])
            for k in range(2):
                half[k, :ny] = out[k * ny:(k + 1) * ny, :nx].astype(BF)
                half[k, ny:] = out[k * ny:(k + 1) * ny, nx:].astype(BF)
            for k in range(2):
                base[way, (d + k) * shots + s] = dot(ymat[way], half[k])
            return carry

        lax.fori_loop(0, shots * depths // 2, two_depths, 0)

    def out_copies(way, d):
        target = so_hbm if way == 0 else ao_hbm
        return pltpu.make_async_copy(field.at[way, :, :, d], target.at[:, :, d], out_sem.at[way, d])

    def grad_copy(d):
        return pltpu.make_async_copy(grad.at[d], g_hbm.at[d], grad_sem.at[d])

    def final_fields(way, with_gradient):
        ey, ex = edge[way, 0:1, : 2 * ny], edge[way, 0:1, 2 * ny:]
        ey_turned = jnp.concatenate([-ey[:, ny:], ey[:, :ny]], axis=1)
        ones = lax.broadcasted_iota(jnp.int32, (8, 1), 0)

        def one_depth(d, carry):
            for s in range(shots):
                now = pq[way, pl.ds(d * shots + s, 1), :]
                p, q = now[:, : 2 * ny], now[:, 2 * ny:]
                turned = jnp.concatenate([-p[:, ny:], p[:, :ny]], axis=1)
                left = jnp.where(
                    ones == 0, p,
                    jnp.where(ones == 1, turned, jnp.where(ones == 2, ey, jnp.where(ones == 3, ey_turned, 0.0))),
                ).astype(BF)
                right = jnp.where(
                    ones == 0, ex[:, :nx],
                    jnp.where(
                        ones == 1, ex[:, nx:],
                        jnp.where(ones == 2, q[:, :nx], jnp.where(ones == 3, q[:, nx:], 0.0)),
                    ),
                ).astype(BF)
                total = (base[way, d * shots + s] + dot_first(left, right)).astype(BF)
                field[way, s, 0, d] = total[:ny]
                field[way, s, 1, d] = total[ny:]
            for side in range(2):
                @pl.when(way == side)
                def _():
                    out_copies(side, d).start()
            if with_gradient:
                acc = jnp.zeros((ny, nx), F32)
                for s in range(shots):
                    acc = acc + field[0, s, 0, d].astype(F32) * field[1, s, 0, d].astype(F32)
                    acc = acc - field[0, s, 1, d].astype(F32) * field[1, s, 1, d].astype(F32)
                grad[d] = acc / shots
                grad_copy(d).start()
            return carry

        lax.fori_loop(0, depths, one_depth, 0)

    state_front = gx + gy
    last_front = n_gx + n_gy - 2
    first = jnp.where(2 * state_front <= last_front, 0, 1)
    second = 1 - first
    early = jnp.minimum(state_front, last_front - state_front)

    local_terms(first)
    pl.semaphore_wait(
        barrier,
        sum(
            (index > 0).astype(jnp.int32) + (index < count - 1).astype(jnp.int32)
            for index, count in ((gx, n_gx), (gy, n_gy), (gz, n_gz))
        ),
    )
    start_both(plane_copies(first))
    local_terms(second)
    start_both(plane_copies(second))
    start_both(halo_copies(first))
    start_both(halo_copies(second))
    wait_arrivals(plane_copies(first))
    averaged_terms(first)
    hop(first)
    wait_arrivals(plane_copies(second))
    averaged_terms(second)

    near_middle = early >= 3

    @pl.when(near_middle)
    def _():
        hop(second)

    wait_arrivals(halo_copies(first))
    base_fields(first)
    final_fields(first, False)
    wait_arrivals(halo_copies(second))
    base_fields(second)

    @pl.when(jnp.logical_not(near_middle))
    def _():
        hop(second)

    final_fields(second, True)
    for way in range(2):
        wait_departures(plane_copies(way))
        wait_departures(halo_copies(way))
        hop_departures(way)
        for d in range(depths):
            out_copies(way, d).wait()
    for d in range(depths):
        grad_copy(d).wait()


def per_device(source_field, adjoint_source, x_inverse, y_inverse):
    shots, _, depths, ny, nx = source_field.shape
    sizes = tuple(lax.axis_size(axis) for axis in ("gx", "gy", "gz"))
    rhs = shots * depths
    wide = 2 * (ny + nx)
    vmem = pltpu.VMEM
    dma = pltpu.SemaphoreType.DMA
    anywhere = pl.BlockSpec(memory_space=pl.ANY)
    return pl.pallas_call(
        functools.partial(kernel, sizes, shots, depths, ny, nx),
        out_shape=(
            jax.ShapeDtypeStruct(source_field.shape, BF),
            jax.ShapeDtypeStruct(source_field.shape, BF),
            jax.ShapeDtypeStruct((depths, ny, nx), F32),
        ),
        in_specs=[anywhere] * 4,
        out_specs=(anywhere,) * 3,
        scratch_shapes=[
            vmem((2, shots, 2, depths + 2, ny, nx), BF),
            vmem((2, nx, nx), BF),
            vmem((2, ny, ny), BF),
            vmem((2, 2 * nx, 2 * nx), BF),
            vmem((2, 2 * ny, 2 * ny), BF),
            vmem((2, 2 * ny, 2 * ny), BF),
            vmem((2, 8, wide), F32),
            vmem((rhs, 2 * ny), F32),
            vmem((rhs, 2 * nx), F32),
            vmem((rhs + 2 * shots, wide), F32),
            vmem((2, rhs, wide), F32),
            vmem((2, 2, shots, wide), F32),
            vmem((2, 2, shots, wide), F32),
            vmem((2, rhs, 2 * ny), BF),
            vmem((2, rhs, 2 * nx), BF),
            vmem((2, rhs, 2 * ny), BF),
            vmem((2, rhs, 2 * nx), BF),
            vmem((2, rhs, wide), F32),
            vmem((2, 2 * ny, nx), BF),
            vmem((2, rhs, 2 * ny, nx), F32),
            vmem((2, shots, 2, depths, ny, nx), BF),
            vmem((depths, ny, nx), F32),
            dma((4,)),
            dma((2, 2)),
            dma((2, 2)),
            dma((2, 2)),
            dma((2, 2)),
            dma((2,)),
            dma((2,)),
            dma((2,)),
            dma((2,)),
            dma((2, depths)),
            dma((depths,)),
        ],
        compiler_params=pltpu.CompilerParams(collective_id=0, has_side_effects=True),
    )(source_field, adjoint_source, x_inverse, y_inverse)


def solution(mesh):
    in_specs = (
        P(None, None, "gz", "gy", "gx"),
        P(None, None, "gz", "gy", "gx"),
        P("gx", "gy", None, None, None),
        P("gx", "gy", None, None, None),
    )
    out_specs = (
        P(None, None, "gz", "gy", "gx"),
        P(None, None, "gz", "gy", "gx"),
        P("gz", "gy", "gx"),
    )
    return jax.shard_map(
        per_device, mesh=mesh, in_specs=in_specs, out_specs=out_specs, check_vma=False
    )
```

time: 298 us -> 40 us (0.13)
  starting transfers between devices: 115 us -> 0 us
  matrix products: 75.2 us -> 0 us
  waiting for transfers between devices: 44.5 us -> 0 us
  other arithmetic: 41.9 us -> 0 us
  Pallas kernels: 0 us -> 34.4 us
  local copies, waits for them, and re-layouts: 15.4 us -> 4.57 us
  loops' own time: 3 us -> 0 us
    ppermute x46 -> x0, starting transfers between devices: 115 us -> none  [the longest x44 110 us: passed_along(): lax.ppermute(value, axis, [(source, source + steps) for source in range(l...]
    dot_general x88 -> x0, matrix products: 75.2 us -> none  [the longest x22 27.1 us: solve_along_x(): jnp.einsum(form, field, real_matrix, preferred_element_type=jnp.float32)]
    ppermute x46 -> x0, waiting for transfers between devices: 44.5 us -> none  [the longest x44 31.2 us: passed_along(): lax.ppermute(value, axis, [(source, source + steps) for source in range(l...]
    pallas_call x0 -> x1, Pallas kernels: none -> 34.4 us  [per_device(): pl.pallas_call(functools.partial(kernel, sizes, shots, depths, ny, nx), o...]
    another operation x45 -> x0, other arithmetic: 32.7 us -> none
    slice x44 -> x0, local copies, waits for them, and re-layouts: 12.2 us -> none  [the longest x11 7.91 us: hand_over(): north_in = passed_along(state_done[:, :, :, row_count - 1, :], 'gy', 1)]
    select_n x22 -> x0, other arithmetic: 4.61 us -> none  [the longest x11 2.32 us: advance(): state_field = jnp.where(state_active, state_new, state_field)]
    unnamed x0 -> x7, local copies, waits for them, and re-layouts: none -> 4.57 us
  transfers between devices with their start and end apart: 46 -> 0, of which waited for: 13 -> 0; matrix products, arithmetic and copies ran while one was open for 23% -> 0% of each run, Pallas kernels for 0% -> 0%
where the time goes in v1:
time: 40 us; the launch traced here: 39.7 us
  Pallas kernels  34.4 us (86%)
  local copies, waits for them, and re-layouts  4.57 us (11%)
  between operations  0.65 us (2%)
    pallas_call x1, Pallas kernels, per_device(): pl.pallas_call(functools.partial(kernel, sizes, shots, depths, ny, nx), o...  34.4 us
    unnamed x7, local copies, waits for them, and re-layouts  4.57 us

profile of v1, /device:TPU:1, one launch (start us, length us, event | category | flops | bytes accessed | tf_op | source)
XLA Modules:
  0.0 39.7 jit_solution(2497879175672558798)
XLA Ops:
  0.6 34.4 %shard_map.67 = (bf16[2,2,4,128,256]{4,3,2,1,0:T(8,128)(2,1)}, bf16[2,2,4,128,256]{4,3,2,1,0:T(8,128)(2,1)}, f32[4,128,256]{2,1,0:T(8,128)}) custom-call(bf16[2,2,4,128,256]{4,3,2,1,0:T(8,128)(2,1)} %s_hbm.1, bf16[2,2,4,128,256]{4,3,2,1,0:T(8,128)(2,1)} %a_hbm.1, bf16[1,1,2,256,256]{4,3,2,1,0:T(8,128)(2,1)} %x_hbm.1, bf16[1,1,2,128,128]{4,3,2,1,0:T(8,128)(2,1)} %y_hbm.1), custom_call_target="tpu_custom_call" | custom-call | tf_op jit(solution)/shard_map/pallas_call | solution.py:396
  35.1 0.0 copy-start
  35.1 2.4 %copy.10 = bf16[2,2,4,128,256]{4,3,2,1,0:T(8,128)(2,1)} copy(bf16[2,2,4,128,256]{4,3,2,1,0:T(8,128)(2,1)} %get-tuple-element.6) | data formatting | bytes 2097152
  37.5 0.0 copy-done
  37.5 0.0 copy-start.1
  37.5 1.0 %copy.11 = bf16[2,2,4,128,256]{4,3,2,1,0:T(8,128)(2,1)} copy(bf16[2,2,4,128,256]{4,3,2,1,0:T(8,128)(2,1)S(1)} %copy-done) | data formatting | bytes 2097152
  38.4 0.4 %copy-done.1 = f32[4,128,256]{2,1,0:T(8,128)S(1)} copy-done((f32[4,128,256]{2,1,0:T(8,128)S(1)}, f32[4,128,256]{2,1,0:T(8,128)}, u32[]{:S(2)}) %copy-start.1) | copy-done | bytes 524312
  38.9 0.8 %copy.12 = f32[4,128,256]{2,1,0:T(8,128)} copy(f32[4,128,256]{2,1,0:T(8,128)S(1)} %copy-done.1) | data formatting | bytes 1048576
Async XLA Ops:
  35.1 2.4 %copy-start = (bf16[2,2,4,128,256]{4,3,2,1,0:T(8,128)(2,1)S(1)}, bf16[2,2,4,128,256]{4,3,2,1,0:T(8,128)(2,1)}, u32[]{:S(2)}) copy-start(bf16[2,2,4,128,256]{4,3,2,1,0:T(8,128)(2,1)} %get-tuple-element.7) | copy-start | bytes 3145732
  37.5 1.4 %copy-start.1 = (f32[4,128,256]{2,1,0:T(8,128)S(1)}, f32[4,128,256]{2,1,0:T(8,128)}, u32[]{:S(2)}) copy-start(f32[4,128,256]{2,1,0:T(8,128)} %get-tuple-element.8) | copy-start | bytes 1572868

commit v2 on v1

--- a/solution.py
+++ b/solution.py
@@ -10,6 +10,7 @@
 MESH = pl.DeviceIdType.MESH
 BF = jnp.bfloat16
 F32 = jnp.float32
+LIMIT = 24 * 1024 * 1024
 
 
 def dot(left, right):
@@ -26,11 +27,11 @@
 
 def kernel(
     sizes, shots, depths, ny, nx,
-    s_hbm, a_hbm, x_hbm, y_hbm, so_hbm, ao_hbm, g_hbm,
-    src, xraw, yraw, xmat, gmat, ymat, edge, sxv, ysv, ext, ab, plane_out, plane_in,
-    c_in, r_in, c_out, r_out, pq, half, base, field, grad,
+    s_hbm, a_hbm, x_hbm, y_hbm, base, pq, edge,
+    src, xraw, yraw, xmat, gmat, ymat, sxv, ysv, ext, ab, plane_out, plane_in,
+    c_in, r_in, c_out, r_out, half,
     load_sem, plane_send, plane_recv, halo_send, halo_recv,
-    c_send, c_recv, r_send, r_recv, out_sem, grad_sem,
+    c_send, c_recv, r_send, r_recv,
 ):
     n_gx, n_gy, n_gz = sizes
     gx, gy, gz = lax.axis_index("gx"), lax.axis_index("gy"), lax.axis_index("gz")
@@ -287,52 +288,6 @@
 
         lax.fori_loop(0, shots * depths // 2, two_depths, 0)
 
-    def out_copies(way, d):
-        target = so_hbm if way == 0 else ao_hbm
-        return pltpu.make_async_copy(field.at[way, :, :, d], target.at[:, :, d], out_sem.at[way, d])
-
-    def grad_copy(d):
-        return pltpu.make_async_copy(grad.at[d], g_hbm.at[d], grad_sem.at[d])
-
-    def final_fields(way, with_gradient):
-        ey, ex = edge[way, 0:1, : 2 * ny], edge[way, 0:1, 2 * ny:]
-        ey_turned = jnp.concatenate([-ey[:, ny:], ey[:, :ny]], axis=1)
-        ones = lax.broadcasted_iota(jnp.int32, (8, 1), 0)
-
-        def one_depth(d, carry):
-            for s in range(shots):
-                now = pq[way, pl.ds(d * shots + s, 1), :]
-                p, q = now[:, : 2 * ny], now[:, 2 * ny:]
-                turned = jnp.concatenate([-p[:, ny:], p[:, :ny]], axis=1)
-                left = jnp.where(
-                    ones == 0, p,
-                    jnp.where(ones == 1, turned, jnp.where(ones == 2, ey, jnp.where(ones == 3, ey_turned, 0.0))),
-                ).astype(BF)
-                right = jnp.where(
-                    ones == 0, ex[:, :nx],
-                    jnp.where(
-                        ones == 1, ex[:, nx:],
-                        jnp.where(ones == 2, q[:, :nx], jnp.where(ones == 3, q[:, nx:], 0.0)),
-                    ),
-                ).astype(BF)
-                total = (base[way, d * shots + s] + dot_first(left, right)).astype(BF)
-                field[way, s, 0, d] = total[:ny]
-                field[way, s, 1, d] = total[ny:]
-            for side in range(2):
-                @pl.when(way == side)
-                def _():
-                    out_copies(side, d).start()
-            if with_gradient:
-                acc = jnp.zeros((ny, nx), F32)
-                for s in range(shots):
-                    acc = acc + field[0, s, 0, d].astype(F32) * field[1, s, 0, d].astype(F32)
-                    acc = acc - field[0, s, 1, d].astype(F32) * field[1, s, 1, d].astype(F32)
-                grad[d] = acc / shots
-                grad_copy(d).start()
-            return carry
-
-        lax.fori_loop(0, depths, one_depth, 0)
-
     state_front = gx + gy
     last_front = n_gx + n_gy - 2
     first = jnp.where(2 * state_front <= last_front, 0, 1)
@@ -366,7 +321,6 @@
 
     wait_arrivals(halo_copies(first))
     base_fields(first)
-    final_fields(first, False)
     wait_arrivals(halo_copies(second))
     base_fields(second)
 
@@ -374,15 +328,37 @@
     def _():
         hop(second)
 
-    final_fields(second, True)
     for way in range(2):
         wait_departures(plane_copies(way))
         wait_departures(halo_copies(way))
         hop_departures(way)
-        for d in range(depths):
-            out_copies(way, d).wait()
-    for d in range(depths):
-        grad_copy(d).wait()
+
+
+def last_kernel(shots, ny, nx, base, pq, edge, state_out, adjoint_out, gradient):
+    d = pl.program_id(0)
+    rows = lax.broadcasted_iota(jnp.int32, (8, 1), 0)
+
+    def stacked(first, second, third, fourth):
+        lower = jnp.where(rows == 2, third, jnp.where(rows == 3, fourth, 0.0))
+        return jnp.where(rows == 0, first, jnp.where(rows == 1, second, lower)).astype(BF)
+
+    for way, out in ((0, state_out), (1, adjoint_out)):
+        ey, ex = edge[way, 0:1, : 2 * ny], edge[way, 0:1, 2 * ny:]
+        ey_turned = jnp.concatenate([-ey[:, ny:], ey[:, :ny]], axis=1)
+        for s in range(shots):
+            now = pq[way, pl.ds(d * shots + s, 1), :]
+            p, q = now[:, : 2 * ny], now[:, 2 * ny:]
+            turned = jnp.concatenate([-p[:, ny:], p[:, :ny]], axis=1)
+            left = stacked(p, turned, ey, ey_turned)
+            right = stacked(ex[:, :nx], ex[:, nx:], q[:, :nx], q[:, nx:])
+            total = (base[way, d * shots + s] + dot_first(left, right)).astype(BF)
+            out[s, 0, 0] = total[:ny]
+            out[s, 1, 0] = total[ny:]
+    acc = jnp.zeros((ny, nx), F32)
+    for s in range(shots):
+        acc = acc + state_out[s, 0, 0].astype(F32) * adjoint_out[s, 0, 0].astype(F32)
+        acc = acc - state_out[s, 1, 0].astype(F32) * adjoint_out[s, 1, 0].astype(F32)
+    gradient[0] = acc / shots
 
 
 def per_device(source_field, adjoint_source, x_inverse, y_inverse):
@@ -392,16 +368,20 @@
     wide = 2 * (ny + nx)
     vmem = pltpu.VMEM
     dma = pltpu.SemaphoreType.DMA
-    anywhere = pl.BlockSpec(memory_space=pl.ANY)
-    return pl.pallas_call(
+    anywhere = pl.BlockSpec(memory_space=pltpu.HBM)
+    operands = [
+        pltpu.with_memory_space_constraint(value, pltpu.HBM)
+        for value in (source_field, adjoint_source, x_inverse, y_inverse)
+    ]
+    base, pq, edge = pl.pallas_call(
         functools.partial(kernel, sizes, shots, depths, ny, nx),
         out_shape=(
-            jax.ShapeDtypeStruct(source_field.shape, BF),
-            jax.ShapeDtypeStruct(source_field.shape, BF),
-            jax.ShapeDtypeStruct((depths, ny, nx), F32),
+            jax.ShapeDtypeStruct((2, rhs, 2 * ny, nx), F32),
+            jax.ShapeDtypeStruct((2, rhs, wide), F32),
+            jax.ShapeDtypeStruct((2, 8, wide), F32),
         ),
         in_specs=[anywhere] * 4,
-        out_specs=(anywhere,) * 3,
+        out_specs=(pl.BlockSpec(memory_space=vmem),) * 3,
         scratch_shapes=[
             vmem((2, shots, 2, depths + 2, ny, nx), BF),
             vmem((2, nx, nx), BF),
@@ -409,7 +389,6 @@
             vmem((2, 2 * nx, 2 * nx), BF),
             vmem((2, 2 * ny, 2 * ny), BF),
             vmem((2, 2 * ny, 2 * ny), BF),
-            vmem((2, 8, wide), F32),
             vmem((rhs, 2 * ny), F32),
             vmem((rhs, 2 * nx), F32),
             vmem((rhs + 2 * shots, wide), F32),
@@ -420,11 +399,7 @@
             vmem((2, rhs, 2 * nx), BF),
             vmem((2, rhs, 2 * ny), BF),
             vmem((2, rhs, 2 * nx), BF),
-            vmem((2, rhs, wide), F32),
             vmem((2, 2 * ny, nx), BF),
-            vmem((2, rhs, 2 * ny, nx), F32),
-            vmem((2, shots, 2, depths, ny, nx), BF),
-            vmem((depths, ny, nx), F32),
             dma((4,)),
             dma((2, 2)),
             dma((2, 2)),
@@ -434,11 +409,24 @@
             dma((2,)),
             dma((2,)),
             dma((2,)),
-            dma((2, depths)),
-            dma((depths,)),
         ],
-        compiler_params=pltpu.CompilerParams(collective_id=0, has_side_effects=True),
-    )(source_field, adjoint_source, x_inverse, y_inverse)
+        compiler_params=pltpu.CompilerParams(
+            collective_id=0, has_side_effects=True, vmem_limit_bytes=LIMIT
+        ),
+    )(*operands)
+    plane = pl.BlockSpec((shots, 2, 1, ny, nx), lambda d: (0, 0, d, 0, 0))
+    return pl.pallas_call(
+        functools.partial(last_kernel, shots, ny, nx),
+        grid=(depths,),
+        out_shape=(
+            jax.ShapeDtypeStruct(source_field.shape, BF),
+            jax.ShapeDtypeStruct(source_field.shape, BF),
+            jax.ShapeDtypeStruct((depths, ny, nx), F32),
+        ),
+        in_specs=[pl.BlockSpec(memory_space=vmem)] * 3,
+        out_specs=(plane, plane, pl.BlockSpec((1, ny, nx), lambda d: (d, 0, 0))),
+        compiler_params=pltpu.CompilerParams(vmem_limit_bytes=LIMIT),
+    )(base, pq, edge)
 
 
 def solution(mesh):

time: 40 us -> 36.6 us (0.915)
  local copies, waits for them, and re-layouts: 4.57 us -> 0 us
  Pallas kernels: 34.4 us -> 35.8 us
    unnamed x7 -> x0, local copies, waits for them, and re-layouts: 4.57 us -> none
    pallas_call x0 -> x1, Pallas kernels: none -> 2.79 us  [per_device(): pl.pallas_call(functools.partial(last_kernel, shots, ny, nx), grid=(depth...]
    pallas_call x1, Pallas kernels: 34.4 us -> 33 us  [per_device(): pl.pallas_call(functools.partial(kernel, sizes, shots, depths, ny, nx), o...]
where the time goes in v2:
time: 36.6 us; the launch traced here: 36.5 us
  Pallas kernels  35.8 us (98%)
  between operations  0.64 us (2%)
    pallas_call x1, Pallas kernels, per_device(): pl.pallas_call(functools.partial(kernel, sizes, shots, depths, ny, nx), o...  33 us
    pallas_call x1, Pallas kernels, per_device(): pl.pallas_call(functools.partial(last_kernel, shots, ny, nx), grid=(depth...  2.79 us

profile of v2, /device:TPU:1, one launch (start us, length us, event | category | flops | bytes accessed | tf_op | source)
XLA Modules:
  0.0 36.5 jit_solution(17508560418364367327)
XLA Ops:
  0.6 33.0 %shard_map.67 = (f32[2,8,256,256]{3,2,1,0:T(8,128)S(1)}, f32[2,8,768]{2,1,0:T(8,128)S(1)}, f32[2,8,768]{2,1,0:T(8,128)S(1)}) custom-call(bf16[2,2,4,128,256]{4,3,2,1,0:T(8,128)(2,1)} %s_hbm.1, bf16[2,2,4,128,256]{4,3,2,1,0:T(8,128)(2,1)} %a_hbm.1, bf16[1,1,2,256,256]{4,3,2,1,0:T(8,128)(2,1)} %x_hbm.1, bf16[1,1,2,128,128]{4,3,2,1,0:T(8,128)(2,1)} %y_hbm.1), custom_call_target="tpu_custom_call" | custom-call | tf_op jit(solution)/shard_map/pallas_call | solution.py:376
  33.7 2.8 %shard_map.68 = (bf16[2,2,4,128,256]{4,3,2,1,0:T(8,128)(2,1)}, bf16[2,2,4,128,256]{4,3,2,1,0:T(8,128)(2,1)}, f32[4,128,256]{2,1,0:T(8,128)}) custom-call(f32[2,8,256,256]{3,2,1,0:T(8,128)S(1)} %get-tuple-element.6.base, f32[2,8,768]{2,1,0:T(8,128)S(1)} %get-tuple-element.7.pq, f32[2,8,768]{2,1,0:T(8,128)S(1)} %get-tuple-element.8.edge), custom_call_target="tpu_custom_call" | custom-call | tf_op jit(solution)/shard_map/pallas_call | solution.py:418
